TPU v7x, 32 devices: a whole 2x2x4 slice. The times are simulated.
32 devices in a mesh: dom: 16 (over z, x, core), sub: 2 (over y).
Axes of the slice: x: 2, y: 2, z: 4, core: 2. Of those that a mesh axis runs over, the one named last changes fastest.
Arguments:
- edge_vectors: float32 [3, 32768], P(None, ('dom', 'sub')), may hold values from -4.95 to 4.95, as said below
- senders: int32 [32768], P(('dom', 'sub')), may hold values from 0 to 175, as said below
- counts: int32 [1024], P(('dom', 'sub')), may hold values from 1 to 32, as said below
- species: int32 [1024], P(('dom', 'sub')), may hold values from 0 to 3
- send_list: int32 [512], P(('dom', 'sub')), may hold values from 0 to 31, as said below
- embed: float32 [128, 4], replicated, may hold values from -6 to 6
- radial_in1: float32 [64, 8], replicated, may hold values from -4 to 4
- radial_mid1: float32 [64, 64], replicated, may hold values from -1.5 to 1.5
- radial_out1: float32 [256, 64], replicated, may hold values from -1.5 to 1.5
- mix_s1: float32 [128, 128], replicated, may hold values from -0.5 to 0.5
- mix_v1: float32 [128, 128], replicated, may hold values from -0.5 to 0.5
- mix_q1: float32 [128, 128], replicated, may hold values from -0.25 to 0.25
- radial_in2: float32 [64, 8], replicated, may hold values from -4 to 4
- radial_mid2: float32 [64, 64], replicated, may hold values from -1.5 to 1.5
- radial_out2: float32 [512, 64], replicated, may hold values from -1.5 to 1.5
- mix_s2: float32 [128, 128], replicated, may hold values from -0.5 to 0.5
- mix_v2: float32 [128, 128], replicated, may hold values from -0.5 to 0.5
- mix_q2: float32 [128, 128], replicated, may hold values from -0.25 to 0.25
- read_lin: float32 [128], replicated, may hold values from -0.5 to 0.5
- read_hidden: float32 [16, 128], replicated, may hold values from -0.5 to 0.5
- read_out: float32 [16], replicated, may hold values from -1.5 to 1.5
Outputs:
- atom_energies: float32 [1024], P(('dom', 'sub'))
- forces: float32 [3, 1024], P(None, ('dom', 'sub'))
Inputs may be any that keep to these rules, and one draw needn't show every extreme that they name: `senders`: A value t of 32 or more names entry (t - 32) % 16 of the send list of the device at offset (s // 3 - 1, s % 3 - 1) along (dom, sub), s = (t - 32) // 16; s is never 4 and never names a device outside the grid. `counts`: an atom's neighbours fill its first slots; the rest are padding. `send_list`: the 16 entries of one device are distinct atoms of that device, counted from its first atom. `edge_vectors`: every column has a length between 0.75 and 4.95.
All inputs are finite; a program needn't handle non-finite values.
Results may differ from a plain program's by a relative error of at most 0.000088.
Values sent between devices are 32-bit elements; how exact they have to be, the bound alone decides.
A program may use at most 64 MiB of HBM per device.

v0:
```python
import math

import jax
import jax.numpy as jnp
from jax import lax
from jax.sharding import PartitionSpec as P

cutoff_radius = 5.0
exact = lax.Precision.HIGHEST


def passed_along(value, axis, steps):
    count = lax.axis_size(axis)
    first, last = (max(0, -steps), min(count, count - steps))
    return lax.ppermute(value, axis, [(source, source + steps) for source in range(first, last)])


def with_halo(block, sides, width):
    for axis, dim in sides:
        count = lax.axis_size(axis)
        forward = [(i, i + 1) for i in range(count - 1)]
        backward = [(target, source) for source, target in forward]
        low = lax.ppermute(
            lax.slice_in_dim(block, block.shape[dim] - width, None, axis=dim), axis, forward
        )
        high = lax.ppermute(lax.slice_in_dim(block, 0, width, axis=dim), axis, backward)
        block = jnp.concatenate([low, block, high], axis=dim)
    return block


def radial_weights(distance, w_in, w_mid, w_out):
    scaled = distance / cutoff_radius
    envelope = 1.0 - 28.0 * scaled**6 + 48.0 * scaled**7 - 21.0 * scaled**8
    harmonic = jnp.arange(1, w_in.shape[1] + 1).astype(distance.dtype)[:, None]
    radial_basis = (
        math.sqrt(2.0 / cutoff_radius)
        * jnp.sin(harmonic * (math.pi / cutoff_radius) * distance[None, :])
        / distance[None, :]
        * envelope[None, :]
    )
    hidden = jax.nn.silu(jnp.dot(w_in, radial_basis, precision=exact))
    hidden = jax.nn.silu(jnp.dot(w_mid, hidden, precision=exact))
    return jnp.dot(w_out, hidden, precision=exact)


def edge_messages(lookup, vectors, sources, live_mask, weights, slots):
    channels = lookup.shape[1]
    edges = vectors.shape[1]
    distance = jnp.sqrt(jnp.sum(vectors * vectors, axis=0))
    unit_dir = vectors / distance[None, :]
    radial = (
        radial_weights(distance, weights[0], weights[1], weights[2]).reshape(-1, channels, edges)
        * live_mask[None, None, :]
    )
    picked = jnp.take(lookup, sources, axis=2)
    scalar = picked[0]
    if lookup.shape[0] == 1:
        scalar_msg = radial[0] * scalar
        vector_msg = radial[1][None] * scalar[None] * unit_dir[:, None, :]
    else:
        vector = picked[1:]
        scalar_msg = radial[0] * scalar + radial[1] * jnp.sum(unit_dir[:, None, :] * vector, axis=0)
        vector_msg = (
            radial[2][None] * scalar[None] * unit_dir[:, None, :] + radial[3][None] * vector
        )
    stacked = jnp.concatenate([scalar_msg[None], vector_msg], axis=0)
    return jnp.sum(stacked.reshape(4, channels, edges // slots, slots), axis=3) * slots ** (-0.5)


def node_update(aggregate, scalar, vector, mix_s, mix_v, mix_q):
    mixed_scalar = jnp.dot(mix_s, aggregate[0], precision=exact)
    mixed_vector = jnp.einsum("cd,kda->kca", mix_v, aggregate[1:], precision=exact)
    squares = mixed_scalar * mixed_scalar + jnp.sum(mixed_vector * mixed_vector, axis=0)
    next_scalar = scalar + mixed_scalar + jnp.dot(mix_q, squares, precision=exact)
    next_vector = vector + mixed_vector + mixed_vector * mixed_scalar[None]
    return (next_scalar, next_vector)


def atom_energy(scalar_one, scalar_two, read_lin, read_hidden, read_out):
    second_term = jnp.dot(
        read_out, jax.nn.silu(jnp.dot(read_hidden, scalar_two, precision=exact)), precision=exact
    )
    return jnp.dot(read_lin, scalar_one, precision=exact) + second_term


def shifted(piece, axis_name, steps):
    if axis_name == "dom":
        return passed_along(piece, "dom", steps)
    return passed_along(piece, "sub", steps)


def reverse_sum(slotted):
    partial_sum = (
        slotted[:, :, 1]
        + shifted(slotted[:, :, 2], "sub", 1)
        + shifted(slotted[:, :, 0], "sub", -1)
    )
    return (
        partial_sum[:, 1]
        + shifted(partial_sum[:, 2], "dom", 1)
        + shifted(partial_sum[:, 0], "dom", -1)
    )


def on_device(
    edge_vectors,
    senders,
    counts,
    species,
    send_list,
    embed,
    radial_in1,
    radial_mid1,
    radial_out1,
    mix_s1,
    mix_v1,
    mix_q1,
    radial_in2,
    radial_mid2,
    radial_out2,
    mix_s2,
    mix_v2,
    mix_q2,
    read_lin,
    read_hidden,
    read_out,
):
    atoms = species.shape[0]
    slots = senders.shape[0] // atoms
    ghosts = send_list.shape[0]
    channels = embed.shape[0]
    block_rows = min(atoms, 32)
    block_count = atoms // block_rows
    live_mask = (jnp.arange(slots)[None, :] < counts[:, None]).reshape(-1).astype(jnp.float32)
    vec_blocks = edge_vectors.reshape(3, block_count, block_rows * slots).transpose(1, 0, 2)
    src_blocks = senders.reshape(block_count, -1)
    mask_blocks = live_mask.reshape(block_count, -1)
    ghost_kinds = with_halo(
        species[send_list].reshape(1, 1, ghosts), (("dom", 0), ("sub", 1)), 1
    ).reshape(-1)
    all_kinds = jnp.concatenate([species, ghost_kinds], axis=0)
    species_hot = (jnp.arange(embed.shape[1])[:, None] == all_kinds[None, :]).astype(jnp.float32)
    initial_table = jnp.dot(embed, species_hot, precision=exact)
    initial = initial_table[:, :atoms]
    layer_one = (radial_in1, radial_mid1, radial_out1)
    layer_two = (radial_in2, radial_mid2, radial_out2)

    def layer_forward(lookup, weights):

        def one_block(block_items):
            return edge_messages(
                lookup, block_items[0], block_items[1], block_items[2], weights, slots
            )

        outputs = lax.map(one_block, (vec_blocks, src_blocks, mask_blocks))
        return outputs.transpose(1, 2, 0, 3).reshape(4, channels, atoms)

    def layer_backward(lookup, weights, upstream):
        up_blocks = upstream.reshape(4, channels, block_count, block_rows).transpose(2, 0, 1, 3)

        def step_fn(carry, block_items):
            vec_block, src_block, mask_block, up_block = block_items

            def local_messages(values, vectors):
                return edge_messages(values, vectors, src_block, mask_block, weights, slots)

            pullback = jax.vjp(local_messages, lookup, vec_block)[1]
            grad_lookup, grad_vectors = pullback(up_block)
            return (carry + grad_lookup, grad_vectors)

        total, grads = lax.scan(
            step_fn, jnp.zeros_like(lookup), (vec_blocks, src_blocks, mask_blocks, up_blocks)
        )
        return (total, grads.transpose(1, 0, 2).reshape(3, -1))

    agg_first = layer_forward(initial_table[None], layer_one)
    zero_vector = jnp.zeros((3, channels, atoms), jnp.float32)
    (scalar_one, vector_one), node_pull = jax.vjp(
        lambda agg_in: node_update(agg_in, initial, zero_vector, mix_s1, mix_v1, mix_q1), agg_first
    )
    features = jnp.concatenate([scalar_one[None], vector_one], axis=0)
    outgoing = jnp.take(features, send_list, axis=2).reshape(4, channels, 1, 1, ghosts)
    ghost_features = with_halo(outgoing, (("dom", 2), ("sub", 3)), 1).reshape(
        4, channels, 9 * ghosts
    )
    lookup_two = jnp.concatenate([features, ghost_features], axis=2)
    agg_second = layer_forward(lookup_two, layer_two)

    def upper(agg_in, scalar_in, vector_in):
        scalar_two = node_update(agg_in, scalar_in, vector_in, mix_s2, mix_v2, mix_q2)[0]
        return atom_energy(scalar_in, scalar_two, read_lin, read_hidden, read_out)

    atom_energies, upper_pull = jax.vjp(upper, agg_second, scalar_one, vector_one)
    grad_agg2, grad_s1, grad_v1 = upper_pull(jnp.ones_like(atom_energies))
    grad_lookup2, grad_edges2 = layer_backward(lookup_two, layer_two, grad_agg2)
    received_two = jnp.sum(grad_edges2.reshape(3, atoms, slots), axis=2)
    sent_two = jnp.zeros((3, atoms + 9 * ghosts), jnp.float32).at[:, senders].add(grad_edges2)
    ghost_grads = grad_lookup2[:, :, atoms:].reshape(4 * channels, 9 * ghosts)
    ghost_back = reverse_sum(ghost_grads.reshape(4 * channels, 3, 3, ghosts)).reshape(
        4, channels, ghosts
    )
    grad_features = grad_lookup2[:, :, :atoms] + jnp.concatenate([grad_s1[None], grad_v1], axis=0)
    grad_features = grad_features.at[:, :, send_list].add(ghost_back)
    grad_agg1 = node_pull((grad_features[0], grad_features[1:]))[0]
    grad_edges1 = layer_backward(initial_table[None], layer_one, grad_agg1)[1]
    received_one = jnp.sum(grad_edges1.reshape(3, atoms, slots), axis=2)
    sent_one = jnp.zeros((3, atoms + 9 * ghosts), jnp.float32).at[:, senders].add(grad_edges1)
    ghost_force = sent_one[:, atoms:] + sent_two[:, atoms:]
    late_force = reverse_sum(ghost_force.reshape(3, 3, 3, ghosts))
    own_sent = sent_one[:, :atoms] + sent_two[:, :atoms]
    own_sent = own_sent.at[:, send_list].add(late_force)
    forces = received_one + received_two - own_sent
    return (atom_energies, forces)


def solution(mesh):
    return jax.shard_map(
        on_device,
        mesh=mesh,
        in_specs=(
            P(None, ("dom", "sub")),
            P(("dom", "sub")),
            P(("dom", "sub")),
            P(("dom", "sub")),
            P(("dom", "sub")),
            P(),
            P(),
            P(),
            P(),
            P(),
            P(),
            P(),
            P(),
            P(),
            P(),
            P(),
            P(),
            P(),
            P(),
            P(),
            P(),
        ),
        out_specs=(P(("dom", "sub")), P(None, ("dom", "sub"))),
        check_vma=False,
    )
```

profile of v0, /device:TPU:3, one launch (start us, length us, event | category | flops | bytes accessed | tf_op | source)
XLA Modules:
  0.0 196.8 jit_solution(14057522713131547557)
XLA Ops:
  2.7 3.7 %collective-permute-start = (s32[1,1,16]{2,1,0:T(1,128)S(1)}, s32[1,1,16]{2,1,0:T(1,128)S(1)}, u32[]{:S(2)}, u32[]{:S(2)}) collective-permute-start(s32[1,1,16]{2,1,0:T(1,128)S(1)} %bitcast.296), channel_id=1, source_target_pairs={{0,2},{2,4},{4,6},{6,8},{8,10},{10,12},{12,14},{14,16},{16,18},{18... | collective-permute-start | bytes 200 | tf_op jit(solution)/shard_map/ppermute | solution.py:23
  6.4 1.9 collective-permute-start.1
  15.1 1.9 fusion.34
  20.5 1.8 fusion.31
  22.6 3.1 %collective-permute-start.2 = (s32[3,1,16]{2,1,0:T(1,128)S(1)}, s32[3,1,16]{2,1,0:T(1,128)S(1)}, u32[]{:S(2)}, u32[]{:S(2)}) collective-permute-start(s32[3,1,16]{2,1,0:T(1,128)S(1)} %pad_add_fusion.1), channel_id=1, source_target_pairs={{0,1},{2,3},{4,5},{6,7},{8,9},{10,11},{12,13},{14,15},{16,17},{18,... | collective-permute-start | bytes 584 | tf_op jit(solution)/shard_map/ppermute | solution.py:23
  27.1 1.8 copy.114
  30.6 2.8 %gather_fusion.1 = f32[1024,128]{1,0:T(8,128)S(1)} fusion(f32[128,176]{0,1:T(8,128)S(1)} %convolution_bitcast_fusion.7, s32[1024]{0:T(1024)S(1)} %get-tuple-element.178), kind=kCustom, calls=%fused_computation.1 | custom fusion | bytes 1052672 | tf_op jit(solution)/shard_map/while/body/eval_jaxpr/jit(_take)/gather | solution.py:55
  38.3 6.0 %collective-permute-start.4 = (f32[4,128,1,1,16]{1,0,4,3,2:T(4,128)S(1)}, f32[4,128,1,1,16]{1,0,4,3,2:T(4,128)S(1)}, u32[]{:S(2)}, u32[]{:S(2)}) collective-permute-start(f32[4,128,1,1,16]{1,0,4,3,2:T(4,128)S(1)} %bitcast_select_fusion.1), channel_id=1, source_target_pairs={{0,2},{2,4},{4,6},{6,8},{8,10},{10,12},{12,14},{14,16},{16,18},{18... | collective-permute-start | bytes 98312 | tf_op jit(solution)/shard_map/ppermute | solution.py:23
  44.3 1.9 collective-permute-start.5
  46.2 4.1 %broadcast_multiply_fusion = f32[4,128,1024]{1,0,2:T(4,128)S(1)} fusion(f32[4,128,1024]{1,0,2:T(4,128)} %copy.114, f32[1024]{0:T(1024)S(1)} %reshape.370), kind=kLoop, calls=%fused_computation.56 | loop fusion | flops 524288 | bytes 4198400 | tf_op jit(solution)/shard_map/while/body/eval_jaxpr/mul | solution.py:52
  50.4 2.0 collective-permute-start.6
  55.0 3.8 %collective-permute-done.7 = f32[4,128,3,1,16]{1,0,4,3,2:T(4,128)S(1)} collective-permute-done((f32[4,128,3,1,16]{1,0,4,3,2:T(4,128)S(1)}, f32[4,128,3,1,16]{1,0,4,3,2:T(4,128)S(1)}, u32[]{:S(2)}, u32[]{:S(2)}) %collective-permute-start.7) | collective-permute-done | bytes 98336 | tf_op jit(solution)/shard_map/ppermute | solution.py:26
  59.0 8.0 %gather_fusion.3 = f32[1024,4,128]{2,1,0:T(4,128)} fusion(f32[4,128,176]{1,0,2:T(4,128)S(1)} %pad_maximum_fusion, s32[1024]{0:T(1024)S(1)} %get-tuple-element.178), kind=kCustom, calls=%fused_computation.3 | custom fusion | bytes 4198400 | tf_op jit(solution)/shard_map/while/body/eval_jaxpr/jit(_take)/gather | solution.py:55
  66.9 5.5 %select_bitcast_fusion = f32[4,128,1024]{1,0,2:T(4,128)S(1)} fusion(f32[1024,4,128]{2,1,0:T(4,128)} %gather_fusion.3, pred[1024]{0:T(1024)(128)(4,1)S(1)} %compare_and_fusion), kind=kLoop, calls=%fused_computation.18 | loop fusion | flops 524288 | bytes 4195328 | tf_op jit(solution)/shard_map/while/body/eval_jaxpr/jit(_take)/select_n | solution.py:55
  72.4 5.7 %multiply_reduce_fusion.5 = f32[128,1024]{0,1:T(8,128)S(1)} fusion(f32[4,128,1024]{1,0,2:T(4,128)S(1)} %select_bitcast_fusion, f32[3,1024]{0,1:T(8,128)S(1)} %copy.143), kind=kLoop, calls=%fused_computation.27 | loop fusion | flops 655360 | bytes 2109440 | tf_op jit(solution)/shard_map/while/body/eval_jaxpr/reduce_sum | solution.py:62
  84.1 3.6 %multiply_reduce_fusion.4 = (f32[128,32,32]{0,2,1:T(8,128)S(1)}, f32[3,32,32]{0,2,1:T(8,128)}) fusion(f32[3,128,32]{1,0,2:T(4,128)S(1)} %copy.122, f32[3,32,32]{0,2,1:T(8,128)S(1)} %bitcast.262, f32[128,32,32]{0,2,1:T(8,128)S(1)} %bitcast.274), kind=kLoop, calls=%fused_computation.25 | loop fusion | flops 1438720 | bytes 1122304 | tf_op jit(solution)/shard_map/while/body/eval_jaxpr/transpose(jvp())/reduce_sum | solution.py:64
  87.8 3.5 %fusion.128 = (f32[1,128,1024]{1,0,2:T(1,128)S(1)}, f32[1,128,1024]{1,0,2:T(1,128)S(1)}, f32[1,128,1024]{1,0,2:T(1,128)}, f32[1,128,1024]{1,0,2:T(1,128)}, f32[1,128,1024]{1,0,2:T(1,128)}) fusion(f32[4,128,1024]{1,0,2:T(4,128)S(1)} %broadcast_multiply_fusion, f32[1,128,1024]{1,0,2:T(1,128)S(1)} %bitcast.267, f32[1,128,1024]{1,0,2:T(1,128)S(1)} %bitcast.281, ...), kind=kLoop, calls=%fused_computation.256 | loop fusion | flops 786432 | bytes 6291456 | tf_op jit(solution)/shard_map/while/body/eval_jaxpr/slice | solution.py:62
  91.4 7.3 %fusion.1 = (f32[128,1024]{0,1:T(8,128)}, f32[3,1024]{0,1:T(8,128)}, f32[3,128,1024]{1,0,2:T(4,128)S(1)}) fusion(f32[4,128,1024]{1,0,2:T(4,128)S(1)} %select_bitcast_fusion, f32[3,128,32]{1,0,2:T(4,128)S(1)} %copy.122, f32[128,1024]{0,1:T(8,128)S(1)} %mul.1033, f32[3,1024]{0,1:T(8,128)S(1)} %copy.143, f32[128,1024]{0,1:T(8,128)S(1)} %bitcast.276), kind=kLoop, calls=%fused_computation.12 | loop fusion | flops 2618368 | bytes 4792320 | tf_op jit(solution)/shard_map/while/body/eval_jaxpr/transpose(jvp())/reduce_sum | solution.py:64
  99.6 33.0 %scatter_fusion = f32[4,128,176]{1,0,2:T(4,128)S(1)} fusion(f32[4,128,176]{1,0,2:T(4,128)S(1)} %broadcast_in_dim.216, s32[1024]{0:T(1024)S(1)} %get-tuple-element.177, f32[1024,4,128]{2,1,0:T(4,128)S(1)} %add_bitcast_fusion), kind=kCustom, calls=%fused_computation.4 | custom fusion | flops 524288 | bytes 6295552 | tf_op jit(solution)/shard_map/while/body/eval_jaxpr/transpose(jvp(jit(_take)))/scatter-add | solution.py:55
  137.0 4.0 %add_multiply_fusion = f32[4,128,1024]{1,0,2:T(4,128)S(1)} fusion(f32[1,128,1024]{1,0,2:T(1,128)S(1)} %copy-done.7, f32[1,128,1024]{1,0,2:T(1,128)S(1)} %copy-done.9, f32[1,128,1024]{1,0,2:T(1,128)S(1)} %copy-done.8, f32[1,128,1024]{1,0,2:T(1,128)} %bitcast.286, f32[1024]{0:T(1024)} %copy-done.32), kind=kLoop, calls=%fused_computation.19 | loop fusion | flops 2097152 | bytes 4198400 | tf_op jit(solution)/shard_map/while/body/eval_jaxpr/transpose(jvp())/mul | solution.py:52
  141.0 2.2 %fusion.5 = f32[64,1024]{1,0:T(8,128)S(1)} fusion(f32[512,64]{0,1:T(8,128)S(1)} %copy-done, f32[128,8,4,128]{3,2,1,0:T(4,128)S(1)} %bitcast.264), kind=kOutput, calls=%fused_computation.29 | convolution fusion | flops 402653184 | bytes 2490368 | tf_op jit(solution)/shard_map/while/body/eval_jaxpr/transpose(jvp())/dot_general | solution.py:43
  144.9 5.2 %collective-permute-start.10 = (f32[512,16]{0,1:T(8,128)S(1)}, f32[512,16]{0,1:T(8,128)S(1)}, u32[]{:S(2)}, u32[]{:S(2)}) collective-permute-start(f32[512,16]{0,1:T(8,128)S(1)} %get-tuple-element.161), channel_id=1, source_target_pairs={{0,2},{2,4},{4,6},{6,8},{8,10},{10,12},{12,14},{14,16},{16,18},{18... | collective-permute-start | bytes 98312 | tf_op jit(solution)/shard_map/ppermute | solution.py:15
  150.1 1.9 collective-permute-start.11
  153.8 2.5 %collective-permute-done.11 = f32[512,16]{0,1:T(8,128)S(1)} collective-permute-done((f32[512,16]{0,1:T(8,128)S(1)}, f32[512,16]{0,1:T(8,128)S(1)}, u32[]{:S(2)}, u32[]{:S(2)}) %collective-permute-start.11) | collective-permute-done | bytes 32800 | tf_op jit(solution)/shard_map/ppermute | solution.py:15
  158.2 2.8 %multiply_reduce_fusion.2 = (f32[128,32,32]{0,2,1:T(8,128)S(1)}, f32[3,32,32]{0,2,1:T(8,128)S(1)}) fusion(f32[3,128,32]{1,0,2:T(4,128)S(1)} %copy.129, f32[3,32,32]{0,2,1:T(8,128)S(1)} %bitcast.263, f32[128,32,32]{0,2,1:T(8,128)S(1)} %bitcast.272), kind=kLoop, calls=%fused_computation.22 | loop fusion | flops 1438720 | bytes 1122304 | tf_op jit(solution)/shard_map/while/body/eval_jaxpr/transpose(jvp())/reduce_sum | solution.py:59
  164.6 6.2 %scatter_custom_fusion.2 = f32[3,176]{0,1:T(8,128)S(1)} fusion(s32[1024]{0:T(1024)} %copy-done.43, f32[1024,3]{1,0:T(8,128)S(1)} %copy.136, f32[]{:T(128)} %constant.243.clone.1), kind=kCustom, calls=%fused_computation.141 | custom fusion | flops 3072 | bytes 2624 | tf_op jit(solution)/shard_map/scatter-add | solution.py:207
  171.0 6.2 %scatter_custom_fusion.3 = f32[3,176]{0,1:T(8,128)S(1)} fusion(s32[1024]{0:T(1024)} %copy-done.43, f32[1024,3]{1,0:T(8,128)S(1)} %copy.137, f32[]{:T(128)} %constant.243.clone.1), kind=kCustom, calls=%fused_computation.139 | custom fusion | flops 3072 | bytes 2624 | tf_op jit(solution)/shard_map/scatter-add | solution.py:197
  177.3 4.3 %collective-permute-start.12 = (f32[3,3,16]{2,0,1:T(4,128)S(1)}, f32[3,3,16]{2,0,1:T(4,128)S(1)}, u32[]{:S(2)}, u32[]{:S(2)}) collective-permute-start(f32[3,3,16]{2,0,1:T(4,128)S(1)} %bitcast.294), channel_id=1, source_target_pairs={{0,1},{2,3},{4,5},{6,7},{8,9},{10,11},{12,13},{14,15},{16,17},{18,... | collective-permute-start | bytes 1736 | tf_op jit(solution)/shard_map/ppermute | solution.py:15
  183.4 2.6 %collective-permute-done.13 = f32[3,3,16]{2,0,1:T(4,128)S(1)} collective-permute-done((f32[3,3,16]{2,0,1:T(4,128)S(1)}, f32[3,3,16]{2,0,1:T(4,128)S(1)}, u32[]{:S(2)}, u32[]{:S(2)}) %collective-permute-start.13) | collective-permute-done | bytes 608 | tf_op jit(solution)/shard_map/ppermute | solution.py:15
  186.0 3.5 %collective-permute-start.14 = (f32[3,16]{1,0:T(4,128)S(1)}, f32[3,16]{1,0:T(4,128)S(1)}, u32[]{:S(2)}, u32[]{:S(2)}) collective-permute-start(f32[3,16]{1,0:T(4,128)S(1)} %get-tuple-element.170), channel_id=1, source_target_pairs={{0,2},{2,4},{4,6},{6,8},{8,10},{10,12},{12,14},{14,16},{16,18},{18... | collective-permute-start | bytes 584 | tf_op jit(solution)/shard_map/ppermute | solution.py:15
  189.6 1.9 collective-permute-start.15
  191.7 3.7 %collective-permute-done.15 = f32[3,16]{1,0:T(4,128)S(1)} collective-permute-done((f32[3,16]{1,0:T(4,128)S(1)}, f32[3,16]{1,0:T(4,128)S(1)}, u32[]{:S(2)}, u32[]{:S(2)}) %collective-permute-start.15) | collective-permute-done | bytes 224 | tf_op jit(solution)/shard_map/ppermute | solution.py:15
  (264 shorter events, 46.0 us)
Async XLA Ops:
  0.6 19.9 %copy-start = (f32[512,64]{0,1:T(8,128)S(1)}, f32[512,64]{0,1:T(8,128)}, u32[]{:S(2)}) copy-start(f32[512,64]{0,1:T(8,128)} %param.35) | copy-start | bytes 393220
  1.3 11.2 %copy-start.47 = (s32[16]{0:T(128)}, s32[16]{0:T(128)S(1)}, u32[]{:S(2)}) copy-start(s32[16]{0:T(128)S(1)} %compare_select_fusion.1) | copy-start | bytes 196
  2.7 19.9 %collective-permute-start = (s32[1,1,16]{2,1,0:T(1,128)S(1)}, s32[1,1,16]{2,1,0:T(1,128)S(1)}, u32[]{:S(2)}, u32[]{:S(2)}) collective-permute-start(s32[1,1,16]{2,1,0:T(1,128)S(1)} %bitcast.296), channel_id=1, source_target_pairs={{0,2},{2,4},{4,6},{6,8},{8,10},{10,12},{12,14},{14,16},{16,18},{18... | collective-permute-start | bytes 200 | tf_op jit(solution)/shard_map/ppermute | solution.py:23
  6.4 16.2 %collective-permute-start.1 = (s32[1,1,16]{2,1,0:T(1,128)S(1)}, s32[1,1,16]{2,1,0:T(1,128)S(1)}, u32[]{:S(2)}, u32[]{:S(2)}) collective-permute-start(s32[1,1,16]{2,1,0:T(1,128)S(1)} %bitcast.297), channel_id=1, source_target_pairs={{2,0},{4,2},{6,4},{8,6},{10,8},{12,10},{14,12},{16,14},{18,16},{20... | collective-permute-start | bytes 200 | tf_op jit(solution)/shard_map/ppermute | solution.py:26
  8.3 9.2 %copy-start.53 = (f32[8]{0:T(128)}, f32[8]{0:T(128)S(1)}, u32[]{:S(2)}) copy-start(f32[8]{0:T(128)S(1)} %convert_multiply_fusion) | copy-start | bytes 100
  9.1 90.5 %copy-start.43 = (s32[1024]{0:T(1024)}, s32[1024]{0:T(1024)S(1)}, u32[]{:S(2)}) copy-start(s32[1024]{0:T(1024)S(1)} %get-tuple-element.177) | copy-start | bytes 12292
  9.8 57.2 %copy-start.40 = (pred[1024]{0:T(1024)(128)(4,1)}, pred[1024]{0:T(1024)(128)(4,1)S(1)}, u32[]{:S(2)}) copy-start(pred[1024]{0:T(1024)(128)(4,1)S(1)} %compare_and_fusion) | copy-start | bytes 3076
  17.6 28.6 %copy-start.32 = (f32[1024]{0:T(1024)}, f32[1024]{0:T(1024)S(1)}, u32[]{:S(2)}) copy-start(f32[1024]{0:T(1024)S(1)} %reshape.370) | copy-start | bytes 12292
  22.6 6.3 %collective-permute-start.2 = (s32[3,1,16]{2,1,0:T(1,128)S(1)}, s32[3,1,16]{2,1,0:T(1,128)S(1)}, u32[]{:S(2)}, u32[]{:S(2)}) collective-permute-start(s32[3,1,16]{2,1,0:T(1,128)S(1)} %pad_add_fusion.1), channel_id=1, source_target_pairs={{0,1},{2,3},{4,5},{6,7},{8,9},{10,11},{12,13},{14,15},{16,17},{18,... | collective-permute-start | bytes 584 | tf_op jit(solution)/shard_map/ppermute | solution.py:23
  25.8 4.3 %collective-permute-start.3 = (s32[3,1,16]{2,1,0:T(1,128)S(1)}, s32[3,1,16]{2,1,0:T(1,128)S(1)}, u32[]{:S(2)}, u32[]{:S(2)}) collective-permute-start(s32[3,1,16]{2,1,0:T(1,128)S(1)} %pad_add_fusion.1), channel_id=1, source_target_pairs={{1,0},{3,2},{5,4},{7,6},{9,8},{11,10},{13,12},{15,14},{17,16},{19,... | collective-permute-start | bytes 584 | tf_op jit(solution)/shard_map/ppermute | solution.py:26
  38.3 15.6 %copy-start.55 = (f32[128]{0:T(128)S(1)}, f32[128]{0:T(128)}, u32[]{:S(2)}) copy-start(f32[128]{0:T(128)} %param.39) | copy-start | bytes 1540
  38.3 12.0 %collective-permute-start.4 = (f32[4,128,1,1,16]{1,0,4,3,2:T(4,128)S(1)}, f32[4,128,1,1,16]{1,0,4,3,2:T(4,128)S(1)}, u32[]{:S(2)}, u32[]{:S(2)}) collective-permute-start(f32[4,128,1,1,16]{1,0,4,3,2:T(4,128)S(1)} %bitcast_select_fusion.1), channel_id=1, source_target_pairs={{0,2},{2,4},{4,6},{6,8},{8,10},{10,12},{12,14},{14,16},{16,18},{18... | collective-permute-start | bytes 98312 | tf_op jit(solution)/shard_map/ppermute | solution.py:23
  44.3 6.1 %collective-permute-start.5 = (f32[4,128,1,1,16]{1,0,4,3,2:T(4,128)S(1)}, f32[4,128,1,1,16]{1,0,4,3,2:T(4,128)S(1)}, u32[]{:S(2)}, u32[]{:S(2)}) collective-permute-start(f32[4,128,1,1,16]{1,0,4,3,2:T(4,128)S(1)} %bitcast_select_fusion.1), channel_id=1, source_target_pairs={{2,0},{4,2},{6,4},{8,6},{10,8},{12,10},{14,12},{16,14},{18,16},{20... | collective-permute-start | bytes 98312 | tf_op jit(solution)/shard_map/ppermute | solution.py:26
  50.4 4.5 %collective-permute-start.6 = (f32[4,128,3,1,16]{1,0,4,3,2:T(4,128)S(1)}, f32[4,128,3,1,16]{1,0,4,3,2:T(4,128)S(1)}, u32[]{:S(2)}, u32[]{:S(2)}) collective-permute-start(f32[4,128,3,1,16]{1,0,4,3,2:T(4,128)S(1)} %pad_maximum_fusion.2), channel_id=1, source_target_pairs={{0,1},{2,3},{4,5},{6,7},{8,9},{10,11},{12,13},{14,15},{16,17},{18,... | collective-permute-start | bytes 294920 | tf_op jit(solution)/shard_map/ppermute | solution.py:23
  52.4 6.4 %collective-permute-start.7 = (f32[4,128,3,1,16]{1,0,4,3,2:T(4,128)S(1)}, f32[4,128,3,1,16]{1,0,4,3,2:T(4,128)S(1)}, u32[]{:S(2)}, u32[]{:S(2)}) collective-permute-start(f32[4,128,3,1,16]{1,0,4,3,2:T(4,128)S(1)} %pad_maximum_fusion.2), channel_id=1, source_target_pairs={{1,0},{3,2},{5,4},{7,6},{9,8},{11,10},{13,12},{15,14},{17,16},{19,... | collective-permute-start | bytes 294920 | tf_op jit(solution)/shard_map/ppermute | solution.py:26
  134.1 10.7 %collective-permute-start.8 = (f32[512,3,16]{0,2,1:T(8,128)S(1)}, f32[512,3,16]{0,2,1:T(8,128)S(1)}, u32[]{:S(2)}, u32[]{:S(2)}) collective-permute-start(f32[512,3,16]{0,2,1:T(8,128)S(1)} %get-tuple-element.159), channel_id=1, source_target_pairs={{0,1},{2,3},{4,5},{6,7},{8,9},{10,11},{12,13},{14,15},{16,17},{18,... | collective-permute-start | bytes 294920 | tf_op jit(solution)/shard_map/ppermute | solution.py:15
  135.4 9.4 %collective-permute-start.9 = (f32[512,3,16]{0,2,1:T(8,128)S(1)}, f32[512,3,16]{0,2,1:T(8,128)S(1)}, u32[]{:S(2)}, u32[]{:S(2)}) collective-permute-start(f32[512,3,16]{0,2,1:T(8,128)S(1)} %get-tuple-element.160), channel_id=1, source_target_pairs={{1,0},{3,2},{5,4},{7,6},{9,8},{11,10},{13,12},{15,14},{17,16},{19,... | collective-permute-start | bytes 294920 | tf_op jit(solution)/shard_map/ppermute | solution.py:15
  143.2 8.8 %copy-start.46 = (f32[16,32]{1,0:T(8,128)S(1)}, f32[16,32]{1,0:T(8,128)}, u32[]{:S(2)}) copy-start(f32[16,32]{1,0:T(8,128)} %copy-done.45) | copy-start | bytes 6148
  143.2 8.8 %copy-start.58 = (f32[32]{0:T(128)S(1)}, f32[32]{0:T(128)}, u32[]{:S(2)}) copy-start(f32[32]{0:T(128)} %convolution_bitcast_fusion.22) | copy-start | bytes 388
  143.3 9.5 %copy-start.11 = (f32[3,1024]{0,1:T(8,128)S(1)}, f32[3,1024]{0,1:T(8,128)}, u32[]{:S(2)}) copy-start(f32[3,1024]{0,1:T(8,128)} %get-tuple-element.97) | copy-start | bytes 36868
  143.3 9.7 %copy-start.10 = (f32[3,32,32]{0,2,1:T(8,128)S(1)}, f32[3,32,32]{0,2,1:T(8,128)}, u32[]{:S(2)}) copy-start(f32[3,32,32]{0,2,1:T(8,128)} %get-tuple-element.101) | copy-start | bytes 36868
  143.8 12.5 %copy-start.48 = (s32[16]{0:T(128)S(1)}, s32[16]{0:T(128)}, u32[]{:S(2)}) copy-start(s32[16]{0:T(128)} %copy-done.47) | copy-start | bytes 196
  143.8 13.9 %copy-start.29 = (f32[128,128]{1,0:T(8,128)S(1)}, f32[128,128]{1,0:T(8,128)}, u32[]{:S(2)}) copy-start(f32[128,128]{1,0:T(8,128)} %param.31) | copy-start | bytes 196612
  144.8 13.1 %copy-start.24 = (f32[128,128]{1,0:T(8,128)S(1)}, f32[128,128]{1,0:T(8,128)}, u32[]{:S(2)}) copy-start(f32[128,128]{1,0:T(8,128)} %param.30) | copy-start | bytes 196612
  144.8 13.3 %copy-start.3 = (f32[1,128,1024]{1,2,0:T(8,128)S(1)}, f32[1,128,1024]{1,2,0:T(8,128)}, u32[]{:S(2)}) copy-start(f32[1,128,1024]{1,2,0:T(8,128)} %copy-done.2) | copy-start | bytes 1572868
  144.9 8.9 %collective-permute-start.10 = (f32[512,16]{0,1:T(8,128)S(1)}, f32[512,16]{0,1:T(8,128)S(1)}, u32[]{:S(2)}, u32[]{:S(2)}) collective-permute-start(f32[512,16]{0,1:T(8,128)S(1)} %get-tuple-element.161), channel_id=1, source_target_pairs={{0,2},{2,4},{4,6},{6,8},{8,10},{10,12},{12,14},{14,16},{16,18},{18... | collective-permute-start | bytes 98312 | tf_op jit(solution)/shard_map/ppermute | solution.py:15
  150.1 6.1 %collective-permute-start.11 = (f32[512,16]{0,1:T(8,128)S(1)}, f32[512,16]{0,1:T(8,128)S(1)}, u32[]{:S(2)}, u32[]{:S(2)}) collective-permute-start(f32[512,16]{0,1:T(8,128)S(1)} %get-tuple-element.162), channel_id=1, source_target_pairs={{2,0},{4,2},{6,4},{8,6},{10,8},{12,10},{14,12},{16,14},{18,16},{20... | collective-permute-start | bytes 98312 | tf_op jit(solution)/shard_map/ppermute | solution.py:15
  163.8 31.6 %copy-start.49 = (s32[16]{0:T(128)S(1)}, s32[16]{0:T(128)}, u32[]{:S(2)}) copy-start(s32[16]{0:T(128)} %copy-done.47) | copy-start | bytes 196
  177.3 6.1 %collective-permute-start.12 = (f32[3,3,16]{2,0,1:T(4,128)S(1)}, f32[3,3,16]{2,0,1:T(4,128)S(1)}, u32[]{:S(2)}, u32[]{:S(2)}) collective-permute-start(f32[3,3,16]{2,0,1:T(4,128)S(1)} %bitcast.294), channel_id=1, source_target_pairs={{0,1},{2,3},{4,5},{6,7},{8,9},{10,11},{12,13},{14,15},{16,17},{18,... | collective-permute-start | bytes 1736 | tf_op jit(solution)/shard_map/ppermute | solution.py:15
  181.7 4.4 %collective-permute-start.13 = (f32[3,3,16]{2,0,1:T(4,128)S(1)}, f32[3,3,16]{2,0,1:T(4,128)S(1)}, u32[]{:S(2)}, u32[]{:S(2)}) collective-permute-start(f32[3,3,16]{2,0,1:T(4,128)S(1)} %bitcast.295), channel_id=1, source_target_pairs={{1,0},{3,2},{5,4},{7,6},{9,8},{11,10},{13,12},{15,14},{17,16},{19,... | collective-permute-start | bytes 1736 | tf_op jit(solution)/shard_map/ppermute | solution.py:15
  186.0 5.6 %collective-permute-start.14 = (f32[3,16]{1,0:T(4,128)S(1)}, f32[3,16]{1,0:T(4,128)S(1)}, u32[]{:S(2)}, u32[]{:S(2)}) collective-permute-start(f32[3,16]{1,0:T(4,128)S(1)} %get-tuple-element.170), channel_id=1, source_target_pairs={{0,2},{2,4},{4,6},{6,8},{8,10},{10,12},{12,14},{14,16},{16,18},{18... | collective-permute-start | bytes 584 | tf_op jit(solution)/shard_map/ppermute | solution.py:15
  189.6 5.8 %collective-permute-start.15 = (f32[3,16]{1,0:T(4,128)S(1)}, f32[3,16]{1,0:T(4,128)S(1)}, u32[]{:S(2)}, u32[]{:S(2)}) collective-permute-start(f32[3,16]{1,0:T(4,128)S(1)} %get-tuple-element.171), channel_id=1, source_target_pairs={{2,0},{4,2},{6,4},{8,6},{10,8},{12,10},{14,12},{16,14},{18,16},{20... | collective-permute-start | bytes 584 | tf_op jit(solution)/shard_map/ppermute | solution.py:15
  (49 other events, 131.8 us)
where the time goes:
time: 198 us; the launch traced here: 197 us
  other arithmetic  99 us (50%)
  starting transfers between devices  42.4 us (21%)
  local copies, waits for them, and re-layouts  22 us (11%)
  matrix products  16.9 us (9%)
  waiting for transfers between devices  14.3 us (7%)
  between operations  2.3 us (1%)
    scatter-add x1, other arithmetic, edge_messages(): picked = jnp.take(lookup, sources, axis=2)  33 us
    ppermute x8, starting transfers between devices, passed_along(): lax.ppermute(value, axis, [(source, source + steps) for source in range(f...  20.9 us
    ppermute x4, starting transfers between devices, with_halo(): lax.ppermute(lax.slice_in_dim(block, block.shape[dim] - width, None, axis...  14.8 us
    scatter-add x2, other arithmetic, on_device(): jnp.zeros((3, atoms + 9 * ghosts), jnp.float32).at[:, senders]  12.3 us
    gather x2, local copies, waits for them, and re-layouts, edge_messages(): picked = jnp.take(lookup, sources, axis=2)  10.8 us
    mul x4, other arithmetic, edge_messages(): radial_weights(distance, weights[0], weights[1], weights[2])  9.47 us
    ppermute x8, waiting for transfers between devices, passed_along(): lax.ppermute(value, axis, [(source, source + steps) for source in range(f...  8.78 us
    reduce_sum x1, other arithmetic, edge_messages(): radial[3][None] * vector  7.29 us
  transfers between devices with their start and end apart: 16, of which 7 were waited for; matrix products, arithmetic and copies ran while one was open for 15% of the time, Pallas kernels for 0%

commit v1 on v0

v1 whole, which is shorter than its diff:
```python
import functools
import math

import jax
import jax.numpy as jnp
from jax import lax
from jax.experimental import pallas as pl
from jax.experimental.pallas import tpu as pltpu
from jax.sharding import PartitionSpec as P

cutoff_radius = 5.0
f32 = jnp.float32
bf16 = jnp.bfloat16
LANES = 128
MESH = pl.DeviceIdType.MESH


def mm(a, b, ca, cb):
    return lax.dot_general(a, b, (((ca,), (cb,)), ((), ())), preferred_element_type=f32)


def split(x):
    hi = x.astype(bf16)
    return hi, (x - hi.astype(f32)).astype(bf16)


def split3(x):
    hi = x.astype(bf16)
    rest = x - hi.astype(f32)
    mid = rest.astype(bf16)
    return hi, mid, (rest - mid.astype(f32)).astype(bf16)


def dot3(a, b, ca, cb):
    a_hi, a_lo = split(a)
    b_hi, b_lo = split(b)
    return mm(a_hi, b_hi, ca, cb) + (mm(a_hi, b_lo, ca, cb) + mm(a_lo, b_hi, ca, cb))


def hot2(hot, x, ca, cb):
    hi, lo = split(x)
    return mm(hot, hi, ca, cb) + mm(hot, lo, ca, cb)


def hot3(hot, x, ca, cb):
    hi, mid, lo = split3(x)
    return mm(hot, hi, ca, cb) + (mm(hot, mid, ca, cb) + mm(hot, lo, ca, cb))


def to_column(row):
    count = row.shape[1]
    shape = (count, count)
    same = lax.broadcasted_iota(jnp.int32, shape, 0) == lax.broadcasted_iota(jnp.int32, shape, 1)
    return jnp.sum(jnp.where(same, row, 0.0), axis=1, keepdims=True)


def series(t, first, terms):
    total = jnp.ones_like(t)
    for i in reversed(range(terms)):
        low = first + 2 * i
        total = 1.0 - t * (1.0 / (low * (low + 1))) * total
    return total


def kernel(
    n_dom,
    n_sub,
    vec_ref,
    senders_ref,
    counts_ref,
    species_ref,
    list_ref,
    embed_ref,
    win1_ref,
    wmid1_ref,
    wout1_ref,
    ms1_ref,
    mv1_ref,
    mq1_ref,
    win2_ref,
    wmid2_ref,
    wout2_ref,
    ms2_ref,
    mv2_ref,
    mq2_ref,
    lin_ref,
    rh_ref,
    ro_ref,
    energy_ref,
    force_ref,
    kinds,
    kinds_out,
    table,
    feat_out,
    grad_table,
    grad_in,
    force_table,
    force_in,
    live_hot,
    spec_hot,
    src_hot,
    v8,
    dbas,
    inv_ref,
    pack,
    rhs,
    winp,
    wmid,
    w1,
    w2,
    hid_ref,
    u_ref,
    ds1_ref,
    ds2_ref,
    rad_ref,
    x_ref,
    sums,
    agg2,
    dagg2,
    dh_ref,
    du_ref,
    gp_hi,
    gp_lo,
    qt,
    send_sem,
    recv_sem,
):
    dm, sb = lax.axis_index("dom"), lax.axis_index("sub")
    atoms = species_ref.shape[1]
    edges = vec_ref.shape[1]
    slots = edges // atoms
    ghosts = list_ref.shape[1]
    channels, kinds_n = embed_ref.shape
    hidden, n_basis = win1_ref.shape
    chunk = 8 * slots
    n_chunks = edges // chunk
    scale = slots ** (-0.5)
    C = channels
    sides = [s for s in range(9) if s != 4]

    def exists(s):
        ok = None
        for here, count, off in ((dm, n_dom, s // 3 - 1), (sb, n_sub, s % 3 - 1)):
            if off == 0:
                continue
            one = here > 0 if off < 0 else here < count - 1
            ok = one if ok is None else jnp.logical_and(ok, one)
        return ok

    def place(s):
        return (dm + (s // 3 - 1), sb + (s % 3 - 1))

    def copy_for(phase, s, src, dst, there):
        return pltpu.make_async_remote_copy(
            src_ref=src,
            dst_ref=dst,
            send_sem=send_sem.at[phase, s],
            recv_sem=recv_sem.at[phase, 8 - s],
            device_id=place(there),
            device_id_type=MESH,
        )

    def ghost_rows(s):
        return pl.ds(atoms + ghosts * s, ghosts)

    def copies(phase, s, there):
        pairs = (
            lambda k, r: (kinds_out, kinds.at[ghost_rows(r)]),
            lambda k, r: (feat_out, table.at[ghost_rows(r)]),
            lambda k, r: (grad_table.at[ghost_rows(k)], grad_in.at[r]),
            lambda k, r: (force_table.at[ghost_rows(k)], force_in.at[r]),
        )
        src, dst = pairs[phase](s, 8 - s)
        return copy_for(phase, s, src, dst, there)

    def send_all(phase):
        for s in sides:
            @pl.when(exists(s))
            def _():
                copies(phase, s, s).start()

    def wait_all(phase):
        for s in sides:
            @pl.when(exists(s))
            def _():
                copies(phase, s, s).wait_send()
                copies(phase, 8 - s, s).wait_recv()

    kinds[...] = jnp.zeros_like(kinds)
    table[...] = jnp.zeros_like(table)
    grad_in[...] = jnp.zeros_like(grad_in)
    force_in[...] = jnp.zeros_like(force_in)
    barrier = pltpu.get_barrier_semaphore()
    for s in sides:
        @pl.when(exists(s))
        def _():
            pl.semaphore_signal(barrier, inc=1, device_id=place(s), device_id_type=MESH)

    species_col = to_column(species_ref[...].astype(f32))
    counts_col = to_column(counts_ref[...].astype(f32)).astype(jnp.int32)
    list_col = to_column(list_ref[...].astype(f32))
    lane_a = lax.broadcasted_iota(jnp.int32, (atoms, LANES), 1).astype(f32)
    own_kinds = (species_col == lane_a).astype(f32)
    kinds[0:atoms, :] = own_kinds
    listed = (
        list_col == lax.broadcasted_iota(jnp.int32, (ghosts, atoms), 1).astype(f32)
    ).astype(f32).astype(bf16)
    kinds_out[...] = mm(listed, own_kinds.astype(bf16), 1, 0)
    near = [
        1 + jnp.where(at > 0, 1, 0) + jnp.where(at < count - 1, 1, 0)
        for at, count in ((dm, n_dom), (sb, n_sub))
    ]
    pl.semaphore_wait(barrier, near[0] * near[1] - 1)
    send_all(0)

    wmid[...] = jnp.zeros_like(wmid)
    wmid[0:hidden, 0:hidden] = wmid1_ref[...]
    wmid[hidden:, hidden:] = wmid2_ref[...]
    w1[...] = jnp.zeros_like(w1)
    w1[:, 0:hidden] = wout1_ref[...]
    w2[...] = jnp.zeros_like(w2)
    w2[:, hidden:] = wout2_ref[...]
    winp[...] = jnp.zeros_like(winp)
    winp[0:hidden, 0:n_basis] = win1_ref[...]
    winp[hidden:, 0:n_basis] = win2_ref[...]
    n_pack = 3 * n_basis
    row_i = lax.broadcasted_iota(jnp.int32, rhs.shape, 0)
    lane_i = lax.broadcasted_iota(jnp.int32, rhs.shape, 1)
    which = jnp.zeros(rhs.shape, f32)
    for k in range(3):
        in_rows = (row_i >= LANES * (k + 1)) & (row_i < LANES * (k + 2))
        for part in range(3):
            which = jnp.where(in_rows & (lane_i == n_pack + 8 * part + k), 1.0, which)
    rhs[...] = which
    for half, w_ref in enumerate((win1_ref, win2_ref)):
        hi, lo = split(w_ref[...])
        rows = slice(half * hidden, (half + 1) * hidden)
        rhs[rows, 0:n_basis] = hi.astype(f32)
        rhs[rows, n_basis : 2 * n_basis] = hi.astype(f32)
        rhs[rows, 2 * n_basis : 3 * n_basis] = lo.astype(f32)

    v8[...] = jnp.zeros_like(v8)
    v8[0:3, :] = vec_ref[...]
    vectors = v8[...]
    dist = jnp.sqrt(jnp.sum(vectors * vectors, axis=0, keepdims=True))
    inv = 1.0 / dist
    unit = vectors * inv
    v8[...] = unit
    inv_ref[...] = inv
    x1 = dist * (1.0 / cutoff_radius)
    x2 = x1 * x1
    x5 = x2 * x2 * x1
    x6 = x5 * x1
    env = 1.0 + x6 * (-28.0 + x1 * (48.0 - 21.0 * x1))
    denv = x5 * (-168.0 + x1 * (336.0 - 168.0 * x1)) * (1.0 / cutoff_radius)
    order = (lax.broadcasted_iota(jnp.int32, (n_basis, edges), 0) + 1).astype(f32)
    turns = order * x1
    near = jnp.floor(turns + 0.5)
    odd = near - 2.0 * jnp.floor(near * 0.5)
    sign = 1.0 - 2.0 * odd
    angle = (turns - near) * math.pi
    t = angle * angle
    sine = sign * angle * series(t, 2, 7)
    cosine = sign * series(t, 1, 7)
    norm = math.sqrt(2.0 / cutoff_radius)
    wave = (norm * inv) * sine
    basis = wave * env
    dbas[...] = ((norm * math.pi / cutoff_radius) * order * cosine * inv - wave * inv) * env + wave * denv

    b_hi, b_lo = split(basis)
    u_hi, u_mid, u_lo = split3(unit)
    parts = [b_hi, b_lo, b_hi, u_hi, u_mid, u_lo]
    pack[...] = jnp.concatenate([p.astype(f32) for p in parts], axis=0).astype(bf16)

    def rows_of(c):
        return pl.ds(pl.multiple_of(c * chunk, chunk), chunk)

    def radial_step(c, _):
        rows = rows_of(c)
        out = mm(pack[:, rows], rhs[...].astype(bf16), 0, 1)
        p1 = out[:, :LANES]
        u_ref[rows, :] = out[:, LANES:]
        s1 = jax.nn.sigmoid(p1)
        h1 = p1 * s1
        ds1_ref[rows, :] = s1 * (1.0 + p1 * (1.0 - s1))
        p2 = dot3(h1, wmid[...], 1, 1)
        s2 = jax.nn.sigmoid(p2)
        hid_ref[rows, :] = p2 * s2
        ds2_ref[rows, :] = s2 * (1.0 + p2 * (1.0 - s2))
        return 0

    lax.fori_loop(0, n_chunks, radial_step, 0)

    edge_i = lax.broadcasted_iota(jnp.int32, (atoms, edges), 1)
    atom_i = lax.broadcasted_iota(jnp.int32, (atoms, edges), 0)
    spot = edge_i - atom_i * slots
    live = ((spot >= 0) & (spot < counts_col)).astype(f32)
    live_hot[...] = live
    live_row = jnp.sum(live, axis=0, keepdims=True)
    entry_i = lax.broadcasted_iota(jnp.int32, src_hot.shape, 0)
    src_hot[...] = jnp.where(entry_i == senders_ref[...], live_row, 0.0).astype(bf16)

    own_kinds = kinds[0:atoms, :]
    spread_i = lax.broadcasted_iota(jnp.int32, (kinds_n * atoms, kinds_n), 0)
    kind_i = lax.broadcasted_iota(jnp.int32, (kinds_n * atoms, kinds_n), 1)
    spread = ((spread_i >= kind_i * atoms) & (spread_i < (kind_i + 1) * atoms)).astype(f32).astype(bf16)
    embed_rows = hot3(spread, embed_ref[...], 1, 1)
    initial = hot3(own_kinds[:, 0:kinds_n].astype(bf16), embed_ref[...], 1, 1)

    wait_all(0)
    seen = mm(kinds[...].astype(bf16), src_hot[...], 0, 0)
    for s in range(kinds_n):
        spec_hot[s * atoms : (s + 1) * atoms, :] = (live_hot[...] * seen[s : s + 1, :]).astype(bf16)

    sums[...] = jnp.zeros_like(sums)

    def first_step(c, _):
        rows = rows_of(c)
        hid = hid_ref[rows, :]
        hot = spec_hot[:, rows]
        sums[:, 0:LANES] += hot2(hot, hid, 1, 0)
        for k in range(3):
            lanes = slice(LANES * (k + 1), LANES * (k + 2))
            sums[:, lanes] += hot2(hot, hid * u_ref[rows, LANES * k : LANES * (k + 1)], 1, 0)
        return 0

    lax.fori_loop(0, n_chunks, first_step, 0)

    def by_kind(x):
        total = x[0:atoms]
        for s in range(1, kinds_n):
            total = total + x[s * atoms : (s + 1) * atoms]
        return total

    agg = []
    for k in range(4):
        weight = w1[0:C, :] if k == 0 else w1[C : 2 * C, :]
        spread_agg = dot3(sums[:, LANES * k : LANES * (k + 1)], weight, 1, 1)
        agg.append(by_kind(spread_agg * embed_rows) * scale)

    def mixed(parts, ms, mv, mq):
        a = dot3(parts[0], ms, 1, 1)
        b = dot3(jnp.concatenate(parts[1:], axis=0), mv, 1, 1)
        b = [b[k * atoms : (k + 1) * atoms] for k in range(3)]
        squares = a * a + (b[0] * b[0] + b[1] * b[1] + b[2] * b[2])
        return a, b, dot3(squares, mq, 1, 1)

    a1, b1, q1 = mixed(agg, ms1_ref[...], mv1_ref[...], mq1_ref[...])
    scalar_one = initial + a1 + q1
    feats = [scalar_one] + [b + b * a1 for b in b1]
    for k in range(4):
        table[0:atoms, C * k : C * (k + 1)] = feats[k]
        feat_out[:, C * k : C * (k + 1)] = hot3(listed, feats[k], 1, 0)
    send_all(1)

    def second_radial(c, _):
        rows = rows_of(c)
        rad_ref[rows, :] = dot3(hid_ref[rows, :], w2[...], 1, 1)
        return 0

    lax.fori_loop(0, n_chunks, second_radial, 0)
    wait_all(1)

    def second_step(c, _):
        rows = rows_of(c)
        x = hot2(src_hot[:, rows], table[...], 0, 0)
        x_ref[rows, :] = x
        s, v = x[:, :C], [x[:, C * k : C * (k + 1)] for k in (1, 2, 3)]
        u = [u_ref[rows, LANES * k : LANES * (k + 1)] for k in range(3)]
        r = [rad_ref[rows, C * k : C * (k + 1)] for k in range(4)]
        uv = u[0] * v[0] + u[1] * v[1] + u[2] * v[2]
        rs = r[2] * s
        msgs = [r[0] * s + r[1] * uv] + [rs * u[k] + r[3] * v[k] for k in range(3)]
        group = pl.ds(pl.multiple_of(c * 8, 8), 8)
        for k in range(4):
            agg2[group, C * k : C * (k + 1)] = jnp.sum(msgs[k].reshape(8, slots, C), axis=1) * scale
        return 0

    lax.fori_loop(0, n_chunks, second_step, 0)

    parts = [agg2[:, C * k : C * (k + 1)] for k in range(4)]
    a2, b2, q2 = mixed(parts, ms2_ref[...], mv2_ref[...], mq2_ref[...])
    scalar_two = scalar_one + a2 + q2
    z = dot3(scalar_two, rh_ref[...], 1, 1)
    sz = jax.nn.sigmoid(z)
    lin8 = jnp.broadcast_to(lin_ref[...], (8, C))
    ro8 = jnp.broadcast_to(ro_ref[...], (8, ro_ref.shape[1]))
    energy = dot3(lin8, scalar_one, 1, 1) + dot3(ro8, z * sz, 1, 1)
    energy_ref[...] = energy[0:1, :]

    dz = ro_ref[...] * (sz * (1.0 + z * (1.0 - sz)))
    ds_two = dot3(dz, rh_ref[...], 1, 0)
    dq = dot3(ds_two, mq2_ref[...], 1, 0)
    da = ds_two + 2.0 * a2 * dq
    dagg2[:, 0:C] = dot3(da, ms2_ref[...], 1, 0) * scale
    db = dot3(jnp.concatenate([2.0 * b * dq for b in b2], axis=0), mv2_ref[...], 1, 0) * scale
    for k in range(3):
        dagg2[:, C * (k + 1) : C * (k + 2)] = db[k * atoms : (k + 1) * atoms]
    ds_direct = ds_two + lin_ref[...]

    def pick_lane(k, rows_n):
        lane = lax.broadcasted_iota(jnp.int32, (rows_n, LANES), 1)
        return (lane == 8 + k).astype(f32).astype(bf16)

    grad_table[...] = jnp.zeros_like(grad_table)

    def second_back(c, _):
        rows = rows_of(c)
        group = pl.ds(pl.multiple_of(c * 8, 8), 8)
        d = []
        for k in range(4):
            small = dagg2[group, C * k : C * (k + 1)]
            d.append(jnp.broadcast_to(small[:, None, :], (8, slots, C)).reshape(chunk, C))
        s, v = x_ref[rows, 0:C], [x_ref[rows, C * k : C * (k + 1)] for k in (1, 2, 3)]
        u = [u_ref[rows, LANES * k : LANES * (k + 1)] for k in range(3)]
        r = [rad_ref[rows, C * k : C * (k + 1)] for k in range(4)]
        uv = u[0] * v[0] + u[1] * v[1] + u[2] * v[2]
        ud = u[0] * d[1] + u[1] * d[2] + u[2] * d[3]
        dv = d[1] * v[0] + d[2] * v[1] + d[3] * v[2]
        drad = jnp.concatenate([d[0] * s, d[0] * uv, s * ud, dv], axis=1)
        dh_ref[rows, :] = dot3(drad, w2[...], 1, 0)
        hot = src_hot[:, rows]
        r1d = r[1] * d[0]
        r2s = r[2] * s
        grad_table[:, 0:C] += hot2(hot, r[0] * d[0] + r[2] * ud, 1, 0)
        du = jnp.zeros((chunk, LANES), f32)
        for k in range(3):
            lanes = slice(C * (k + 1), C * (k + 2))
            grad_table[:, lanes] += hot2(hot, r1d * u[k] + r[3] * d[k + 1], 1, 0)
            hi, lo = split(r1d * v[k] + r2s * d[k + 1])
            pick = pick_lane(k, C)
            du = du + (mm(hi, pick, 1, 0) + mm(lo, pick, 1, 0))
        du_ref[rows, :] = du
        return 0

    lax.fori_loop(0, n_chunks, second_back, 0)
    send_all(2)
    wait_all(2)
    ghost_grad = grad_in[0]
    for s in range(1, 9):
        ghost_grad = ghost_grad + grad_in[s]
    dfeat = grad_table[0:atoms, :] + hot3(listed, ghost_grad, 0, 0)
    ds = dfeat[:, 0:C] + ds_direct
    dv = [dfeat[:, C * k : C * (k + 1)] for k in (1, 2, 3)]
    dq = dot3(ds, mq1_ref[...], 1, 0)
    da = ds + 2.0 * a1 * dq + (dv[0] * b1[0] + dv[1] * b1[1] + dv[2] * b1[2])
    db = [dv[k] * (1.0 + a1) + 2.0 * b1[k] * dq for k in range(3)]
    dagg = [dot3(da, ms1_ref[...], 1, 0) * scale]
    db = dot3(jnp.concatenate(db, axis=0), mv1_ref[...], 1, 0) * scale
    dagg += [db[k * atoms : (k + 1) * atoms] for k in range(3)]
    for k in range(4):
        weight = w1[0:C, :] if k == 0 else w1[C : 2 * C, :]
        spread_grad = jnp.concatenate([dagg[k]] * kinds_n, axis=0) * embed_rows
        hi, lo = split(dot3(spread_grad, weight, 1, 0))
        gp_hi[:, LANES * k : LANES * (k + 1)] = hi
        gp_lo[:, LANES * k : LANES * (k + 1)] = lo

    def first_back(c, _):
        rows = rows_of(c)
        hot = spec_hot[:, rows]
        g = mm(hot, gp_hi[...], 0, 0) + mm(hot, gp_lo[...], 0, 0)
        hid = hid_ref[rows, :]
        dh = dh_ref[rows, :] + g[:, 0:LANES]
        q = du_ref[rows, :]
        for k in range(3):
            gk = g[:, LANES * (k + 1) : LANES * (k + 2)]
            dh = dh + u_ref[rows, LANES * k : LANES * (k + 1)] * gk
            hi, lo = split(hid * gk)
            pick = pick_lane(k, LANES)
            q = q + (mm(hi, pick, 1, 0) + mm(lo, pick, 1, 0))
        dp2 = dh * ds2_ref[rows, :]
        dp1 = dot3(dp2, wmid[...], 1, 0) * ds1_ref[rows, :]
        q = q + dot3(dp1, winp[...], 1, 0)
        qt[:, rows] = jnp.transpose(q)
        return 0

    lax.fori_loop(0, n_chunks, first_back, 0)

    unit = v8[...]
    inv = inv_ref[...]
    dr = jnp.sum(qt[0:n_basis, :] * dbas[...], axis=0, keepdims=True)
    du = qt[8:16, :]
    along = jnp.sum(unit * du, axis=0, keepdims=True)
    g8 = dr * unit + (du - unit * along) * inv
    g_hi, g_mid, g_lo = split3(g8)
    hot = src_hot[...]
    force_table[...] = jnp.zeros_like(force_table)
    force_table[:, 0:8] = mm(hot, g_hi, 1, 1) + (mm(hot, g_mid, 1, 1) + mm(hot, g_lo, 1, 1))
    send_all(3)
    own = (live_hot[...] - src_hot[0:atoms, :].astype(f32)).astype(bf16)
    force = mm(g_hi, own, 1, 1) + (mm(g_mid, own, 1, 1) + mm(g_lo, own, 1, 1))
    wait_all(3)
    ghost_force = force_in[0]
    for s in range(1, 9):
        ghost_force = ghost_force + force_in[s]
    hi, mid, lo = split3(ghost_force)
    late = mm(hi, listed, 0, 0) + (mm(mid, listed, 0, 0) + mm(lo, listed, 0, 0))
    force_ref[...] = (force - late[0:8, :])[0:3, :]


def on_device(n_dom, n_sub, *args):
    (vec, senders, counts, species, send_list, embed) = args[:6]
    weights = list(args[6:18])
    read_lin, read_hidden, read_out = args[18:]
    edges = vec.shape[1]
    atoms = species.shape[0]
    ghosts = send_list.shape[0]
    channels, kinds_n = embed.shape
    hidden, n_basis = weights[0].shape
    entries = -(-(atoms + 9 * ghosts) // LANES) * LANES
    wide = 4 * channels
    row = lambda x: x.reshape(1, -1)
    scratch = [
        ((entries, LANES), f32),
        ((ghosts, LANES), f32),
        ((entries, wide), f32),
        ((ghosts, wide), f32),
        ((entries, wide), f32),
        ((9, ghosts, wide), f32),
        ((entries, LANES), f32),
        ((9, ghosts, LANES), f32),
        ((atoms, edges), f32),
        ((kinds_n * atoms, edges), bf16),
        ((entries, edges), bf16),
        ((8, edges), f32),
        ((n_basis, edges), f32),
        ((1, edges), f32),
        ((3 * n_basis + 24, edges), bf16),
        ((4 * LANES, 3 * n_basis + 24), f32),
        ((LANES, LANES), f32),
        ((LANES, LANES), f32),
        ((2 * channels, LANES), f32),
        ((4 * channels, LANES), f32),
        ((edges, LANES), f32),
        ((edges, 3 * LANES), f32),
        ((edges, LANES), f32),
        ((edges, LANES), f32),
        ((edges, wide), f32),
        ((edges, wide), f32),
        ((kinds_n * atoms, 4 * LANES), f32),
        ((atoms, wide), f32),
        ((atoms, wide), f32),
        ((edges, LANES), f32),
        ((edges, LANES), f32),
        ((kinds_n * atoms, 4 * LANES), bf16),
        ((kinds_n * atoms, 4 * LANES), bf16),
        ((LANES, edges), f32),
    ]
    whole = pl.BlockSpec(memory_space=pltpu.VMEM)
    energy, force = pl.pallas_call(
        functools.partial(kernel, n_dom, n_sub),
        out_shape=(
            jax.ShapeDtypeStruct((1, atoms), f32),
            jax.ShapeDtypeStruct((3, atoms), f32),
        ),
        in_specs=[whole] * 21,
        out_specs=(whole, whole),
        scratch_shapes=[pltpu.VMEM(shape, dtype) for shape, dtype in scratch]
        + [pltpu.SemaphoreType.DMA((4, 9)), pltpu.SemaphoreType.DMA((4, 9))],
        compiler_params=pltpu.CompilerParams(
            collective_id=0, has_side_effects=True, vmem_limit_bytes=56 * 1024 * 1024
        ),
    )(
        vec,
        row(senders),
        row(counts),
        row(species),
        row(send_list),
        embed,
        *weights,
        row(read_lin),
        read_hidden,
        row(read_out),
    )
    return energy.reshape(-1), force


def solution(mesh):
    one = P(("dom", "sub"))
    return jax.shard_map(
        functools.partial(on_device, mesh.shape["dom"], mesh.shape["sub"]),
        mesh=mesh,
        in_specs=(P(None, ("dom", "sub")), one, one, one, one) + (P(),) * 16,
        out_specs=(one, P(None, ("dom", "sub"))),
        check_vma=False,
    )
```

time: 198 us -> 39.7 us (0.20)
  other arithmetic: 99 us -> 0 us
  starting transfers between devices: 42.4 us -> 0 us
  Pallas kernels: 0 us -> 32.7 us
  matrix products: 16.9 us -> 0 us
  local copies, waits for them, and re-layouts: 22 us -> 6.1 us
  waiting for transfers between devices: 14.3 us -> 0 us
    scatter-add x5 -> x0, other arithmetic: 47.1 us -> none  [the longest x1 33 us: edge_messages(): picked = jnp.take(lookup, sources, axis=2)]
    ppermute x16 -> x0, starting transfers between devices: 42.4 us -> none  [the longest x8 20.9 us: passed_along(): lax.ppermute(value, axis, [(source, source + steps) for source in range(f...]
    pallas_call x0 -> x1, Pallas kernels: none -> 32.7 us  [on_device(): pl.pallas_call(functools.partial(kernel, n_dom, n_sub), out_shape=(jax.Sh...]
    reduce_sum x11 -> x0, other arithmetic: 22.3 us -> none  [the longest x1 7.29 us: edge_messages(): radial[3][None] * vector]
    dot_general x29 -> x0, matrix products: 16.9 us -> none  [the longest x4 6.7 us: radial_weights(): return jnp.dot(w_out, hidden, precision=exact)]
    ppermute x16 -> x0, waiting for transfers between devices: 14.3 us -> none  [the longest x8 8.78 us: passed_along(): lax.ppermute(value, axis, [(source, source + steps) for source in range(f...]
    gather x4 -> x0, local copies, waits for them, and re-layouts: 12.7 us -> none  [the longest x2 10.8 us: edge_messages(): picked = jnp.take(lookup, sources, axis=2)]
    mul x14 -> x0, other arithmetic: 11.4 us -> none  [the longest x4 9.47 us: edge_messages(): radial_weights(distance, weights[0], weights[1], weights[2])]
  transfers between devices with their start and end apart: 16 -> 0, of which waited for: 7 -> 0; matrix products, arithmetic and copies ran while one was open for 15% -> 0% of each run, Pallas kernels for 0% -> 0%
where the time goes in v1:
time: 39.7 us; the launch traced here: 39.5 us
  Pallas kernels  32.7 us (82%)
  local copies, waits for them, and re-layouts  6.1 us (15%)
  between operations  0.68 us (2%)
    pallas_call x1, Pallas kernels, on_device(): pl.pallas_call(functools.partial(kernel, n_dom, n_sub), out_shape=(jax.Sh...  32.7 us
    unnamed x21, local copies, waits for them, and re-layouts  6.1 us

profile of v1, /device:TPU:3, one launch (start us, length us, event | category | flops | bytes accessed | tf_op | source)
XLA Modules:
  0.0 39.5 jit_solution(12843233490486035480)
XLA Ops:
  0.6 0.0 copy-start.2
  0.6 0.0 copy-start.3
  0.7 0.7 %copy-done.2 = f32[64,8]{0,1:T(8,128)S(1)} copy-done((f32[64,8]{0,1:T(8,128)S(1)}, f32[64,8]{0,1:T(8,128)}, u32[]{:S(2)}) %copy-start.2) | copy-done | bytes 2072
  1.3 0.0 copy-start.1
  1.3 0.7 %copy.24.win1_ref = f32[64,8]{1,0:T(8,128)} copy(f32[64,8]{0,1:T(8,128)S(1)} %copy-done.2) | data formatting | bytes 4096 | tf_op args[6]
  2.0 0.0 copy-done.3
  2.0 0.0 copy-start.4
  2.0 0.7 %copy.26.win2_ref = f32[64,8]{1,0:T(8,128)} copy(f32[64,8]{0,1:T(8,128)S(1)} %copy-done.3) | data formatting | bytes 4096 | tf_op args[12]
  2.7 0.0 copy-done.4
  2.7 0.0 copy-start
  2.7 0.7 %copy.23.embed_ref = f32[128,4]{1,0:T(8,128)} copy(f32[128,4]{0,1:T(4,128)S(1)} %copy-done.4) | data formatting | bytes 4096 | tf_op args[5]
  3.4 0.0 copy-done.1
  3.4 0.8 %copy.25.wout1_ref = f32[256,64]{1,0:T(8,128)} copy(f32[256,64]{0,1:T(8,128)S(1)} %copy-done.1) | data formatting | bytes 131072 | tf_op args[8]
  4.2 0.0 copy-done
  4.2 0.8 %copy.27.wout2_ref = f32[512,64]{1,0:T(8,128)} copy(f32[512,64]{0,1:T(8,128)S(1)} %copy-done) | data formatting | bytes 262144 | tf_op args[14]
  5.0 32.7 %shard_map.212 = (f32[1,32]{1,0:T(1,128)}, f32[3,32]{1,0:T(4,128)}) custom-call(f32[3,1024]{1,0:T(4,128)} %vec_ref.1, s32[1,1024]{1,0:T(1,128)} %bitcast.7, s32[1,32]{1,0:T(1,128)} %bitcast.8, s32[1,32]{1,0:T(1,128)} %bitcast.9, s32[1,16]{1,0:T(1,128)} %bitcast.10, f32[128,4]{1,0:T(8,128)} %copy.23.embed_ref, f32[64,8]{1,0:T(8,128)} %copy.24.win1_ref, ...), custom_call_target="tpu_custom_call" | custom-call | tf_op jit(solution)/shard_map/pallas_call | solution.py:550
  37.8 0.0 copy-start.6
  37.8 0.0 copy-start.5
  37.8 0.6 %copy-done.6 = f32[1,32]{1,0:T(1,128)S(1)} copy-done((f32[1,32]{1,0:T(1,128)S(1)}, f32[1,32]{1,0:T(1,128)}, u32[]{:S(2)}) %copy-start.6) | copy-done | bytes 152
  38.4 0.5 %copy.30 = f32[32]{0:T(128)} copy(f32[32]{0:T(128)S(1)} %bitcast.13) | data formatting | bytes 256
  38.9 0.0 copy-done.5
  38.9 0.6 %copy.31 = f32[3,32]{1,0:T(4,128)} copy(f32[3,32]{1,0:T(4,128)S(1)} %copy-done.5) | data formatting | bytes 768
Async XLA Ops:
  0.6 0.7 %copy-start.2 = (f32[64,8]{0,1:T(8,128)S(1)}, f32[64,8]{0,1:T(8,128)}, u32[]{:S(2)}) copy-start(f32[64,8]{0,1:T(8,128)} %param.27) | copy-start | bytes 6148
  0.6 1.4 %copy-start.3 = (f32[64,8]{0,1:T(8,128)S(1)}, f32[64,8]{0,1:T(8,128)}, u32[]{:S(2)}) copy-start(f32[64,8]{0,1:T(8,128)} %param.33) | copy-start | bytes 6148
  1.3 2.1 %copy-start.1 = (f32[256,64]{0,1:T(8,128)S(1)}, f32[256,64]{0,1:T(8,128)}, u32[]{:S(2)}) copy-start(f32[256,64]{0,1:T(8,128)} %param.29) | copy-start | bytes 196612
  2.0 0.7 %copy-start.4 = (f32[128,4]{0,1:T(4,128)S(1)}, f32[128,4]{0,1:T(4,128)}, u32[]{:S(2)}) copy-start(f32[128,4]{0,1:T(4,128)} %param.26) | copy-start | bytes 6148
  2.7 1.5 %copy-start = (f32[512,64]{0,1:T(8,128)S(1)}, f32[512,64]{0,1:T(8,128)}, u32[]{:S(2)}) copy-start(f32[512,64]{0,1:T(8,128)} %param.35) | copy-start | bytes 393220
  37.8 0.7 %copy-start.6 = (f32[1,32]{1,0:T(1,128)S(1)}, f32[1,32]{1,0:T(1,128)}, u32[]{:S(2)}) copy-start(f32[1,32]{1,0:T(1,128)} %get-tuple-element.4) | copy-start | bytes 388
  37.8 1.2 %copy-start.5 = (f32[3,32]{1,0:T(4,128)S(1)}, f32[3,32]{1,0:T(4,128)}, u32[]{:S(2)}) copy-start(f32[3,32]{1,0:T(4,128)} %get-tuple-element.9) | copy-start | bytes 1156

commit v2 on v1

--- a/solution.py
+++ b/solution.py
@@ -104,10 +104,14 @@
     inv_ref,
     pack,
     rhs,
+    wide_rhs,
     winp,
+    winp_k,
     wmid,
+    wmid_f,
+    wmid_b,
     w1,
-    w2,
+    w2_k,
     hid_ref,
     u_ref,
     ds1_ref,
@@ -119,8 +123,7 @@
     dagg2,
     dh_ref,
     du_ref,
-    gp_hi,
-    gp_lo,
+    gp,
     qt,
     send_sem,
     recv_sem,
@@ -130,8 +133,8 @@
     edges = vec_ref.shape[1]
     slots = edges // atoms
     ghosts = list_ref.shape[1]
-    channels, kinds_n = embed_ref.shape
-    hidden, n_basis = win1_ref.shape
+    kinds_n, channels = embed_ref.shape
+    n_basis, hidden = win1_ref.shape
     chunk = 8 * slots
     n_chunks = edges // chunk
     scale = slots ** (-0.5)
@@ -216,28 +219,45 @@
     wmid[...] = jnp.zeros_like(wmid)
     wmid[0:hidden, 0:hidden] = wmid1_ref[...]
     wmid[hidden:, hidden:] = wmid2_ref[...]
+    hi, lo = split(wmid[...])
+    wmid_f[...] = jnp.concatenate([hi, hi, lo], axis=1)
+    wmid_b[...] = jnp.concatenate([hi, hi, lo], axis=0)
     w1[...] = jnp.zeros_like(w1)
-    w1[:, 0:hidden] = wout1_ref[...]
-    w2[...] = jnp.zeros_like(w2)
-    w2[:, hidden:] = wout2_ref[...]
+    w1[0:hidden, :] = wout1_ref[...]
+    hi, lo = split(wout2_ref[...])
+    w2_k[...] = jnp.concatenate([lo, hi, jnp.zeros_like(hi), hi], axis=0)
     winp[...] = jnp.zeros_like(winp)
-    winp[0:hidden, 0:n_basis] = win1_ref[...]
-    winp[hidden:, 0:n_basis] = win2_ref[...]
+    winp[0:n_basis, 0:hidden] = win1_ref[...]
+    winp[0:n_basis, hidden:] = win2_ref[...]
+    hi, lo = split(winp[...])
+    winp_k[...] = jnp.concatenate([hi, hi, lo], axis=1)
     n_pack = 3 * n_basis
     row_i = lax.broadcasted_iota(jnp.int32, rhs.shape, 0)
     lane_i = lax.broadcasted_iota(jnp.int32, rhs.shape, 1)
     which = jnp.zeros(rhs.shape, f32)
     for k in range(3):
-        in_rows = (row_i >= LANES * (k + 1)) & (row_i < LANES * (k + 2))
+        in_lanes = (lane_i >= LANES * (k + 1)) & (lane_i < LANES * (k + 2))
         for part in range(3):
-            which = jnp.where(in_rows & (lane_i == n_pack + 8 * part + k), 1.0, which)
+            which = jnp.where(in_lanes & (row_i == n_pack + 8 * part + k), 1.0, which)
     rhs[...] = which
-    for half, w_ref in enumerate((win1_ref, win2_ref)):
-        hi, lo = split(w_ref[...])
-        rows = slice(half * hidden, (half + 1) * hidden)
-        rhs[rows, 0:n_basis] = hi.astype(f32)
-        rhs[rows, n_basis : 2 * n_basis] = hi.astype(f32)
-        rhs[rows, 2 * n_basis : 3 * n_basis] = lo.astype(f32)
+    hi, lo = split(winp[0:n_basis, :])
+    rhs[0:n_basis, 0:LANES] = hi.astype(f32)
+    rhs[n_basis : 2 * n_basis, 0:LANES] = hi.astype(f32)
+    rhs[2 * n_basis : 3 * n_basis, 0:LANES] = lo.astype(f32)
+    wide_rhs[...] = rhs[...].astype(bf16)
+
+    def dot_k(a, stacked, dim):
+        a_hi, a_lo = split(a)
+        both = jnp.concatenate([a_hi, a_lo], axis=1)
+        if dim == 1:
+            first, last = stacked[:, : 2 * LANES], stacked[:, 2 * LANES :]
+        else:
+            first, last = stacked[: 2 * LANES, :], stacked[2 * LANES :, :]
+        return mm(both, first, 1, dim) + mm(a_hi, last, 1, dim)
+
+    def upper_half(x, other):
+        lane = lax.broadcasted_iota(jnp.int32, x.shape, 1)
+        return jnp.where(lane >= hidden, x, other)
 
     v8[...] = jnp.zeros_like(v8)
     v8[0:3, :] = vec_ref[...]
@@ -277,13 +297,13 @@
 
     def radial_step(c, _):
         rows = rows_of(c)
-        out = mm(pack[:, rows], rhs[...].astype(bf16), 0, 1)
+        out = mm(pack[:, rows], wide_rhs[...], 0, 0)
         p1 = out[:, :LANES]
         u_ref[rows, :] = out[:, LANES:]
         s1 = jax.nn.sigmoid(p1)
         h1 = p1 * s1
         ds1_ref[rows, :] = s1 * (1.0 + p1 * (1.0 - s1))
-        p2 = dot3(h1, wmid[...], 1, 1)
+        p2 = dot_k(h1, wmid_f, 1)
         s2 = jax.nn.sigmoid(p2)
         hid_ref[rows, :] = p2 * s2
         ds2_ref[rows, :] = s2 * (1.0 + p2 * (1.0 - s2))
@@ -304,24 +324,24 @@
     spread_i = lax.broadcasted_iota(jnp.int32, (kinds_n * atoms, kinds_n), 0)
     kind_i = lax.broadcasted_iota(jnp.int32, (kinds_n * atoms, kinds_n), 1)
     spread = ((spread_i >= kind_i * atoms) & (spread_i < (kind_i + 1) * atoms)).astype(f32).astype(bf16)
-    embed_rows = hot3(spread, embed_ref[...], 1, 1)
-    initial = hot3(own_kinds[:, 0:kinds_n].astype(bf16), embed_ref[...], 1, 1)
+    embed_rows = hot3(spread, embed_ref[...], 1, 0)
+    initial = hot3(own_kinds[:, 0:kinds_n].astype(bf16), embed_ref[...], 1, 0)
 
     wait_all(0)
     seen = mm(kinds[...].astype(bf16), src_hot[...], 0, 0)
     for s in range(kinds_n):
-        spec_hot[s * atoms : (s + 1) * atoms, :] = (live_hot[...] * seen[s : s + 1, :]).astype(bf16)
+        hot = (live_hot[...] * seen[s : s + 1, :]).astype(bf16)
+        spec_hot[s * atoms : (s + 1) * atoms, :] = hot
+        spec_hot[(kinds_n + s) * atoms : (kinds_n + s + 1) * atoms, :] = hot
 
     sums[...] = jnp.zeros_like(sums)
 
     def first_step(c, _):
         rows = rows_of(c)
         hid = hid_ref[rows, :]
-        hot = spec_hot[:, rows]
-        sums[:, 0:LANES] += hot2(hot, hid, 1, 0)
-        for k in range(3):
-            lanes = slice(LANES * (k + 1), LANES * (k + 2))
-            sums[:, lanes] += hot2(hot, hid * u_ref[rows, LANES * k : LANES * (k + 1)], 1, 0)
+        hot = spec_hot[0 : kinds_n * atoms, rows]
+        turned = [hid * u_ref[rows, LANES * k : LANES * (k + 1)] for k in range(3)]
+        sums[...] += hot2(hot, jnp.concatenate([hid] + turned, axis=1), 1, 0)
         return 0
 
     lax.fori_loop(0, n_chunks, first_step, 0)
@@ -334,8 +354,8 @@
 
     agg = []
     for k in range(4):
-        weight = w1[0:C, :] if k == 0 else w1[C : 2 * C, :]
-        spread_agg = dot3(sums[:, LANES * k : LANES * (k + 1)], weight, 1, 1)
+        weight = w1[:, 0:C] if k == 0 else w1[:, C : 2 * C]
+        spread_agg = dot3(sums[:, LANES * k : LANES * (k + 1)], weight, 1, 0)
         agg.append(by_kind(spread_agg * embed_rows) * scale)
 
     def mixed(parts, ms, mv, mq):
@@ -355,7 +375,10 @@
 
     def second_radial(c, _):
         rows = rows_of(c)
-        rad_ref[rows, :] = dot3(hid_ref[rows, :], w2[...], 1, 1)
+        hid = hid_ref[rows, :]
+        twice = upper_half(hid, pltpu.roll(hid, hidden, 1)).astype(bf16)
+        rest = split(hid)[1]
+        rad_ref[rows, :] = mm(jnp.concatenate([twice, rest], axis=1), w2_k[...], 1, 0)
         return 0
 
     lax.fori_loop(0, n_chunks, second_radial, 0)
@@ -398,43 +421,56 @@
         dagg2[:, C * (k + 1) : C * (k + 2)] = db[k * atoms : (k + 1) * atoms]
     ds_direct = ds_two + lin_ref[...]
 
-    def pick_lane(k, rows_n):
-        lane = lax.broadcasted_iota(jnp.int32, (rows_n, LANES), 1)
-        return (lane == 8 + k).astype(f32).astype(bf16)
+    def lane_sum(k, x):
+        lane = lax.broadcasted_iota(jnp.int32, x.shape, 1)
+        return jnp.where(lane == 8 + k, jnp.sum(x, axis=1, keepdims=True), 0.0)
 
     grad_table[...] = jnp.zeros_like(grad_table)
+
+    def spread_rows(c):
+        group = pl.ds(pl.multiple_of(c * 8, 8), 8)
+        out = []
+        for k in range(4):
+            small = dagg2[group, C * k : C * (k + 1)]
+            out.append(jnp.broadcast_to(small[:, None, :], (8, slots, C)).reshape(chunk, C))
+        return out
+
+    def second_scatter(c, _):
+        rows = rows_of(c)
+        d = spread_rows(c)
+        u = [u_ref[rows, LANES * k : LANES * (k + 1)] for k in range(3)]
+        r = [rad_ref[rows, C * k : C * (k + 1)] for k in range(4)]
+        ud = u[0] * d[1] + u[1] * d[2] + u[2] * d[3]
+        r1d = r[1] * d[0]
+        dx = [r[0] * d[0] + r[2] * ud] + [r1d * u[k] + r[3] * d[k + 1] for k in range(3)]
+        grad_table[...] += hot2(src_hot[:, rows], jnp.concatenate(dx, axis=1), 1, 0)
+        return 0
+
+    lax.fori_loop(0, n_chunks, second_scatter, 0)
+    send_all(2)
 
     def second_back(c, _):
         rows = rows_of(c)
-        group = pl.ds(pl.multiple_of(c * 8, 8), 8)
-        d = []
-        for k in range(4):
-            small = dagg2[group, C * k : C * (k + 1)]
-            d.append(jnp.broadcast_to(small[:, None, :], (8, slots, C)).reshape(chunk, C))
+        d = spread_rows(c)
         s, v = x_ref[rows, 0:C], [x_ref[rows, C * k : C * (k + 1)] for k in (1, 2, 3)]
         u = [u_ref[rows, LANES * k : LANES * (k + 1)] for k in range(3)]
-        r = [rad_ref[rows, C * k : C * (k + 1)] for k in range(4)]
         uv = u[0] * v[0] + u[1] * v[1] + u[2] * v[2]
         ud = u[0] * d[1] + u[1] * d[2] + u[2] * d[3]
         dv = d[1] * v[0] + d[2] * v[1] + d[3] * v[2]
         drad = jnp.concatenate([d[0] * s, d[0] * uv, s * ud, dv], axis=1)
-        dh_ref[rows, :] = dot3(drad, w2[...], 1, 0)
-        hot = src_hot[:, rows]
-        r1d = r[1] * d[0]
-        r2s = r[2] * s
-        grad_table[:, 0:C] += hot2(hot, r[0] * d[0] + r[2] * ud, 1, 0)
-        du = jnp.zeros((chunk, LANES), f32)
-        for k in range(3):
-            lanes = slice(C * (k + 1), C * (k + 2))
-            grad_table[:, lanes] += hot2(hot, r1d * u[k] + r[3] * d[k + 1], 1, 0)
-            hi, lo = split(r1d * v[k] + r2s * d[k + 1])
-            pick = pick_lane(k, C)
-            du = du + (mm(hi, pick, 1, 0) + mm(lo, pick, 1, 0))
+        hi, lo = split(drad)
+        dh = mm(hi, w2_k[0:LANES, :], 1, 1)
+        dh = dh + pltpu.roll(dh, hidden, 1) + mm(lo, w2_k[LANES:, :], 1, 1)
+        dh_ref[rows, :] = upper_half(dh, 0.0)
+        r1d = rad_ref[rows, C : 2 * C] * d[0]
+        r2s = rad_ref[rows, 2 * C : 3 * C] * s
+        du = lane_sum(0, r1d * v[0] + r2s * d[1])
+        for k in (1, 2):
+            du = du + lane_sum(k, r1d * v[k] + r2s * d[k + 1])
         du_ref[rows, :] = du
         return 0
 
     lax.fori_loop(0, n_chunks, second_back, 0)
-    send_all(2)
     wait_all(2)
     ghost_grad = grad_in[0]
     for s in range(1, 9):
@@ -449,28 +485,25 @@
     db = dot3(jnp.concatenate(db, axis=0), mv1_ref[...], 1, 0) * scale
     dagg += [db[k * atoms : (k + 1) * atoms] for k in range(3)]
     for k in range(4):
-        weight = w1[0:C, :] if k == 0 else w1[C : 2 * C, :]
+        weight = w1[:, 0:C] if k == 0 else w1[:, C : 2 * C]
         spread_grad = jnp.concatenate([dagg[k]] * kinds_n, axis=0) * embed_rows
-        hi, lo = split(dot3(spread_grad, weight, 1, 0))
-        gp_hi[:, LANES * k : LANES * (k + 1)] = hi
-        gp_lo[:, LANES * k : LANES * (k + 1)] = lo
+        hi, lo = split(dot3(spread_grad, weight, 1, 1))
+        gp[:, LANES * k : LANES * (k + 1)] = jnp.concatenate([hi, lo], axis=0)
 
     def first_back(c, _):
         rows = rows_of(c)
         hot = spec_hot[:, rows]
-        g = mm(hot, gp_hi[...], 0, 0) + mm(hot, gp_lo[...], 0, 0)
+        g = mm(hot, gp[...], 0, 0)
         hid = hid_ref[rows, :]
         dh = dh_ref[rows, :] + g[:, 0:LANES]
         q = du_ref[rows, :]
         for k in range(3):
             gk = g[:, LANES * (k + 1) : LANES * (k + 2)]
             dh = dh + u_ref[rows, LANES * k : LANES * (k + 1)] * gk
-            hi, lo = split(hid * gk)
-            pick = pick_lane(k, LANES)
-            q = q + (mm(hi, pick, 1, 0) + mm(lo, pick, 1, 0))
+            q = q + lane_sum(k, hid * gk)
         dp2 = dh * ds2_ref[rows, :]
-        dp1 = dot3(dp2, wmid[...], 1, 0) * ds1_ref[rows, :]
-        q = q + dot3(dp1, winp[...], 1, 0)
+        dp1 = dot_k(dp2, wmid_b, 0) * ds1_ref[rows, :]
+        q = q + dot_k(dp1, winp_k, 1)
         qt[:, rows] = jnp.transpose(q)
         return 0
 
@@ -506,7 +539,9 @@
     atoms = species.shape[0]
     ghosts = send_list.shape[0]
     channels, kinds_n = embed.shape
-    hidden, n_basis = weights[0].shape
+    n_basis = weights[0].shape[1]
+    for i in (0, 2, 6, 8):
+        weights[i] = weights[i].T
     entries = -(-(atoms + 9 * ghosts) // LANES) * LANES
     wide = 4 * channels
     row = lambda x: x.reshape(1, -1)
@@ -520,17 +555,21 @@
         ((entries, LANES), f32),
         ((9, ghosts, LANES), f32),
         ((atoms, edges), f32),
-        ((kinds_n * atoms, edges), bf16),
+        ((2 * kinds_n * atoms, edges), bf16),
         ((entries, edges), bf16),
         ((8, edges), f32),
         ((n_basis, edges), f32),
         ((1, edges), f32),
         ((3 * n_basis + 24, edges), bf16),
-        ((4 * LANES, 3 * n_basis + 24), f32),
+        ((3 * n_basis + 24, 4 * LANES), f32),
+        ((3 * n_basis + 24, 4 * LANES), bf16),
         ((LANES, LANES), f32),
+        ((LANES, 3 * LANES), bf16),
         ((LANES, LANES), f32),
-        ((2 * channels, LANES), f32),
-        ((4 * channels, LANES), f32),
+        ((LANES, 3 * LANES), bf16),
+        ((3 * LANES, LANES), bf16),
+        ((LANES, 2 * channels), f32),
+        ((2 * LANES, wide), bf16),
         ((edges, LANES), f32),
         ((edges, 3 * LANES), f32),
         ((edges, LANES), f32),
@@ -542,8 +581,7 @@
         ((atoms, wide), f32),
         ((edges, LANES), f32),
         ((edges, LANES), f32),
-        ((kinds_n * atoms, 4 * LANES), bf16),
-        ((kinds_n * atoms, 4 * LANES), bf16),
+        ((2 * kinds_n * atoms, 4 * LANES), bf16),
         ((LANES, edges), f32),
     ]
     whole = pl.BlockSpec(memory_space=pltpu.VMEM)
@@ -566,7 +604,7 @@
         row(counts),
         row(species),
         row(send_list),
-        embed,
+        embed.T,
         *weights,
         row(read_lin),
         read_hidden,

time: 39.7 us -> 32.5 us (0.82)
  local copies, waits for them, and re-layouts: 6.1 us -> 1.71 us
  Pallas kernels: 32.7 us -> 29.9 us
    unnamed x21 -> x6, local copies, waits for them, and re-layouts: 6.1 us -> 1.71 us
    pallas_call x1, Pallas kernels: 32.7 us -> 29.9 us  [on_device(): pl.pallas_call(functools.partial(kernel, n_dom, n_sub), out_shape=(jax.Sh...]
where the time goes in v2:
time: 32.5 us; the launch traced here: 32.3 us
  Pallas kernels  29.9 us (92%)
  local copies, waits for them, and re-layouts  1.71 us (5%)
  between operations  0.66 us (2%)
    pallas_call x1, Pallas kernels, on_device(): pl.pallas_call(functools.partial(kernel, n_dom, n_sub), out_shape=(jax.Sh...  29.9 us
    unnamed x6, local copies, waits for them, and re-layouts  1.71 us

profile of v2, /device:TPU:3, one launch (start us, length us, event | category | flops | bytes accessed | tf_op | source)
XLA Modules:
  0.0 32.3 jit_solution(515238861285356277)
XLA Ops:
  0.6 29.9 %shard_map.212 = (f32[1,32]{1,0:T(1,128)}, f32[3,32]{1,0:T(4,128)}) custom-call(f32[3,1024]{1,0:T(4,128)} %vec_ref.1, s32[1,1024]{1,0:T(1,128)} %bitcast.14, s32[1,32]{1,0:T(1,128)} %bitcast.18, s32[1,32]{1,0:T(1,128)} %bitcast.19, s32[1,16]{1,0:T(1,128)} %bitcast.20, f32[4,128]{1,0:T(4,128)} %bitcast.17, f32[8,64]{1,0:T(8,128)} %bitcast.15, ...), custom_call_target="tpu_custom_call" | custom-call | tf_op jit(solution)/shard_map/pallas_call | solution.py:588
  30.6 0.0 copy-start.1
  30.6 0.0 copy-start
  30.6 0.6 %copy-done.1 = f32[1,32]{1,0:T(1,128)S(1)} copy-done((f32[1,32]{1,0:T(1,128)S(1)}, f32[1,32]{1,0:T(1,128)}, u32[]{:S(2)}) %copy-start.1) | copy-done | bytes 152
  31.2 0.5 %copy.25 = f32[32]{0:T(128)} copy(f32[32]{0:T(128)S(1)} %bitcast.23) | data formatting | bytes 256
  31.7 0.0 copy-done
  31.7 0.6 %copy.26 = f32[3,32]{1,0:T(4,128)} copy(f32[3,32]{1,0:T(4,128)S(1)} %copy-done) | data formatting | bytes 768
Async XLA Ops:
  30.6 0.6 %copy-start.1 = (f32[1,32]{1,0:T(1,128)S(1)}, f32[1,32]{1,0:T(1,128)}, u32[]{:S(2)}) copy-start(f32[1,32]{1,0:T(1,128)} %get-tuple-element.4) | copy-start | bytes 388
  30.6 1.1 %copy-start = (f32[3,32]{1,0:T(4,128)S(1)}, f32[3,32]{1,0:T(4,128)}, u32[]{:S(2)}) copy-start(f32[3,32]{1,0:T(4,128)} %get-tuple-element.9) | copy-start | bytes 1156

commit v3 on v2

--- a/solution.py
+++ b/solution.py
@@ -86,8 +86,7 @@
     lin_ref,
     rh_ref,
     ro_ref,
-    energy_ref,
-    force_ref,
+    out_ref,
     kinds,
     kinds_out,
     table,
@@ -209,12 +208,6 @@
         list_col == lax.broadcasted_iota(jnp.int32, (ghosts, atoms), 1).astype(f32)
     ).astype(f32).astype(bf16)
     kinds_out[...] = mm(listed, own_kinds.astype(bf16), 1, 0)
-    near = [
-        1 + jnp.where(at > 0, 1, 0) + jnp.where(at < count - 1, 1, 0)
-        for at, count in ((dm, n_dom), (sb, n_sub))
-    ]
-    pl.semaphore_wait(barrier, near[0] * near[1] - 1)
-    send_all(0)
 
     wmid[...] = jnp.zeros_like(wmid)
     wmid[0:hidden, 0:hidden] = wmid1_ref[...]
@@ -287,13 +280,24 @@
     basis = wave * env
     dbas[...] = ((norm * math.pi / cutoff_radius) * order * cosine * inv - wave * inv) * env + wave * denv
 
+    peers = [
+        1 + jnp.where(at > 0, 1, 0) + jnp.where(at < count - 1, 1, 0)
+        for at, count in ((dm, n_dom), (sb, n_sub))
+    ]
+    pl.semaphore_wait(barrier, peers[0] * peers[1] - 1)
+    send_all(0)
+
     b_hi, b_lo = split(basis)
     u_hi, u_mid, u_lo = split3(unit)
     parts = [b_hi, b_lo, b_hi, u_hi, u_mid, u_lo]
     pack[...] = jnp.concatenate([p.astype(f32) for p in parts], axis=0).astype(bf16)
 
     def rows_of(c):
-        return pl.ds(pl.multiple_of(c * chunk, chunk), chunk)
+        return slice(c * chunk, (c + 1) * chunk)
+
+    def each_chunk(step):
+        for c in range(n_chunks):
+            step(c, 0)
 
     def radial_step(c, _):
         rows = rows_of(c)
@@ -309,7 +313,7 @@
         ds2_ref[rows, :] = s2 * (1.0 + p2 * (1.0 - s2))
         return 0
 
-    lax.fori_loop(0, n_chunks, radial_step, 0)
+    each_chunk(radial_step)
 
     edge_i = lax.broadcasted_iota(jnp.int32, (atoms, edges), 1)
     atom_i = lax.broadcasted_iota(jnp.int32, (atoms, edges), 0)
@@ -344,7 +348,7 @@
         sums[...] += hot2(hot, jnp.concatenate([hid] + turned, axis=1), 1, 0)
         return 0
 
-    lax.fori_loop(0, n_chunks, first_step, 0)
+    each_chunk(first_step)
 
     def by_kind(x):
         total = x[0:atoms]
@@ -381,7 +385,7 @@
         rad_ref[rows, :] = mm(jnp.concatenate([twice, rest], axis=1), w2_k[...], 1, 0)
         return 0
 
-    lax.fori_loop(0, n_chunks, second_radial, 0)
+    each_chunk(second_radial)
     wait_all(1)
 
     def second_step(c, _):
@@ -394,12 +398,12 @@
         uv = u[0] * v[0] + u[1] * v[1] + u[2] * v[2]
         rs = r[2] * s
         msgs = [r[0] * s + r[1] * uv] + [rs * u[k] + r[3] * v[k] for k in range(3)]
-        group = pl.ds(pl.multiple_of(c * 8, 8), 8)
+        group = slice(c * 8, (c + 1) * 8)
         for k in range(4):
             agg2[group, C * k : C * (k + 1)] = jnp.sum(msgs[k].reshape(8, slots, C), axis=1) * scale
         return 0
 
-    lax.fori_loop(0, n_chunks, second_step, 0)
+    each_chunk(second_step)
 
     parts = [agg2[:, C * k : C * (k + 1)] for k in range(4)]
     a2, b2, q2 = mixed(parts, ms2_ref[...], mv2_ref[...], mq2_ref[...])
@@ -409,7 +413,7 @@
     lin8 = jnp.broadcast_to(lin_ref[...], (8, C))
     ro8 = jnp.broadcast_to(ro_ref[...], (8, ro_ref.shape[1]))
     energy = dot3(lin8, scalar_one, 1, 1) + dot3(ro8, z * sz, 1, 1)
-    energy_ref[...] = energy[0:1, :]
+    out_ref[3:4, :] = energy[0:1, :]
 
     dz = ro_ref[...] * (sz * (1.0 + z * (1.0 - sz)))
     ds_two = dot3(dz, rh_ref[...], 1, 0)
@@ -428,7 +432,7 @@
     grad_table[...] = jnp.zeros_like(grad_table)
 
     def spread_rows(c):
-        group = pl.ds(pl.multiple_of(c * 8, 8), 8)
+        group = slice(c * 8, (c + 1) * 8)
         out = []
         for k in range(4):
             small = dagg2[group, C * k : C * (k + 1)]
@@ -446,7 +450,7 @@
         grad_table[...] += hot2(src_hot[:, rows], jnp.concatenate(dx, axis=1), 1, 0)
         return 0
 
-    lax.fori_loop(0, n_chunks, second_scatter, 0)
+    each_chunk(second_scatter)
     send_all(2)
 
     def second_back(c, _):
@@ -470,7 +474,7 @@
         du_ref[rows, :] = du
         return 0
 
-    lax.fori_loop(0, n_chunks, second_back, 0)
+    each_chunk(second_back)
     wait_all(2)
     ghost_grad = grad_in[0]
     for s in range(1, 9):
@@ -507,7 +511,7 @@
         qt[:, rows] = jnp.transpose(q)
         return 0
 
-    lax.fori_loop(0, n_chunks, first_back, 0)
+    each_chunk(first_back)
 
     unit = v8[...]
     inv = inv_ref[...]
@@ -528,7 +532,7 @@
         ghost_force = ghost_force + force_in[s]
     hi, mid, lo = split3(ghost_force)
     late = mm(hi, listed, 0, 0) + (mm(mid, listed, 0, 0) + mm(lo, listed, 0, 0))
-    force_ref[...] = (force - late[0:8, :])[0:3, :]
+    out_ref[0:3, :] = (force - late[0:8, :])[0:3, :]
 
 
 def on_device(n_dom, n_sub, *args):
@@ -585,14 +589,11 @@
         ((LANES, edges), f32),
     ]
     whole = pl.BlockSpec(memory_space=pltpu.VMEM)
-    energy, force = pl.pallas_call(
+    out = pl.pallas_call(
         functools.partial(kernel, n_dom, n_sub),
-        out_shape=(
-            jax.ShapeDtypeStruct((1, atoms), f32),
-            jax.ShapeDtypeStruct((3, atoms), f32),
-        ),
+        out_shape=jax.ShapeDtypeStruct((4, atoms), f32),
         in_specs=[whole] * 21,
-        out_specs=(whole, whole),
+        out_specs=whole,
         scratch_shapes=[pltpu.VMEM(shape, dtype) for shape, dtype in scratch]
         + [pltpu.SemaphoreType.DMA((4, 9)), pltpu.SemaphoreType.DMA((4, 9))],
         compiler_params=pltpu.CompilerParams(
@@ -610,7 +611,7 @@
         read_hidden,
         row(read_out),
     )
-    return energy.reshape(-1), force
+    return out[3], out[0:3]
 
 
 def solution(mesh):

time: 32.5 us -> 29.8 us (0.917)
  Pallas kernels: 29.9 us -> 27.1 us
    pallas_call x1, Pallas kernels: 29.9 us -> 27.1 us  [on_device(): pl.pallas_call(functools.partial(kernel, n_dom, n_sub), out_shape=jax.Sha...]
    squeeze x0 -> x1, local copies, waits for them, and re-layouts: none -> 1.25 us  [on_device(): return (out[3], out[0:3])]
    unnamed x6 -> x3, local copies, waits for them, and re-layouts: 1.71 us -> 0.58 us
where the time goes in v3:
time: 29.8 us; the launch traced here: 29.6 us
  Pallas kernels  27.1 us (91%)
  local copies, waits for them, and re-layouts  1.83 us (6%)
  between operations  0.66 us (2%)
    pallas_call x1, Pallas kernels, on_device(): pl.pallas_call(functools.partial(kernel, n_dom, n_sub), out_shape=jax.Sha...  27.1 us
    squeeze x1, local copies, waits for them, and re-layouts, on_device(): return (out[3], out[0:3])  1.25 us

profile of v3, /device:TPU:3, one launch (start us, length us, event | category | flops | bytes accessed | tf_op | source)
XLA Modules:
  0.0 29.6 jit_solution(15322013589132316101)
XLA Ops:
  0.6 27.1 %shard_map.212 = f32[4,32]{1,0:T(4,128)} custom-call(f32[3,1024]{1,0:T(4,128)} %vec_ref.1, s32[1,1024]{1,0:T(1,128)} %bitcast.17, s32[1,32]{1,0:T(1,128)} %bitcast.21, s32[1,32]{1,0:T(1,128)} %bitcast.22, s32[1,16]{1,0:T(1,128)} %bitcast.23, f32[4,128]{1,0:T(4,128)} %bitcast.20, f32[8,64]{1,0:T(8,128)} %bitcast.18, f32[64,64]{1,0:T(8,128)} %wmid1_ref.1, ...), custom_call_target="tpu_custom_call" | custom-call | tf_op jit(solution)/shard_map/pallas_call | solution.py:592
  27.7 0.0 copy-start
  27.8 1.2 %slice_bitcast_fusion = f32[32]{0:T(128)} fusion(f32[4,32]{1,0:T(4,128)} %shard_map.212), kind=kLoop, calls=%fused_computation | loop fusion | bytes 256 | tf_op jit(solution)/shard_map/squeeze | solution.py:614
  29.0 0.0 copy-done
  29.0 0.6 %copy.24 = f32[3,32]{1,0:T(4,128)} copy(f32[3,32]{1,0:T(4,128)S(1)} %bitcast.16) | data formatting | bytes 768
Async XLA Ops:
  27.7 1.3 %copy-start = (f32[4,32]{1,0:T(4,128)S(1)}, f32[4,32]{1,0:T(4,128)}, u32[]{:S(2)}) copy-start(f32[4,32]{1,0:T(4,128)} %shard_map.212) | copy-start | bytes 1540
